TPU v7x, 512 devices: a whole 4x4x16 slice. The times are simulated.
512 devices in a mesh: wide: 64 (over x, z), narrow: 8 (over y, core).
Axes of the slice: x: 4, y: 4, z: 16, core: 2. Of those that a mesh axis runs over, the one named last changes fastest.
Arguments:
- velocity: bfloat16 [16, 3, 64, 8, 4, 512], P(None, None, 'wide', 'narrow'), may hold values from -160 to 160
- extents: float32 [3, 64, 8, 4], P(None, 'wide', 'narrow'), may hold values from 0.5 to 2
Outputs:
- q_basis: bfloat16 [16, 3, 64, 8, 4, 512], P(None, None, 'wide', 'narrow')
- r_factor: float32 [16, 16], replicated
- dmd_operator: float32 [16, 15], replicated
All inputs are finite; a program needn't handle non-finite values.
Results may differ from a plain program's by a relative error of at most 0.0055.
Values sent between devices are 32-bit elements; how exact they have to be, the bound alone decides.
No kernel may reach another device: no remote copies, remote signals or barrier semaphores. Data moves between devices by JAX's collectives and lax.ppermute only.
A program may use at most 128 MiB of HBM per device.

v0:
```python
import functools
import math

import jax
import jax.numpy as jnp
import numpy as np
from jax import lax
from jax.experimental import pallas as pl
from jax.experimental.pallas import tpu as pltpu
from jax.sharding import Mesh
from jax.sharding import PartitionSpec as P

WIDE = ("wide_0", "wide_1")
NARROW = ("narrow_0", "narrow_1")
NEAR = ("wide_0", "narrow_0", "narrow_1")
FAR = ("wide_1",)

F32 = jnp.float32
BF16 = jnp.bfloat16
SNAPS = 16
RADIAL = 4
SLABS = 3 * RADIAL
ROWS = SLABS * SNAPS
NODES = 512
HALF = ROWS // 2
Z_ROWS = HALF + 8
Y_ROWS = HALF + 24
VMEM_BYTES = 16 << 20


def gll_tables():
    degree = 7
    node_count = 8
    gll_nodes = np.cos(np.pi * np.arange(node_count) / degree)
    legendre = np.zeros((node_count, node_count))
    for _ in range(60):
        previous = gll_nodes.copy()
        legendre[:, 0] = 1.0
        legendre[:, 1] = previous
        for power in range(2, node_count):
            legendre[:, power] = (
                (2 * power - 1) * previous * legendre[:, power - 1]
                - (power - 1) * legendre[:, power - 2]
            ) / power
        gll_nodes = previous - (previous * legendre[:, degree] - legendre[:, degree - 1]) / (
            node_count * legendre[:, degree]
        )
    legendre[:, 0] = 1.0
    legendre[:, 1] = gll_nodes
    for power in range(2, node_count):
        legendre[:, power] = (
            (2 * power - 1) * gll_nodes * legendre[:, power - 1]
            - (power - 1) * legendre[:, power - 2]
        ) / power
    top_poly = legendre[:, degree][::-1]
    weights = (2.0 / (degree * node_count * legendre[:, degree] ** 2))[::-1]
    ordered = gll_nodes[::-1]
    unit_diag = np.eye(node_count)
    spacing = ordered[:, None] - ordered[None, :] + unit_diag
    derivative = top_poly[:, None] / top_poly[None, :] / spacing
    derivative = derivative * (1.0 - unit_diag)
    derivative[0, 0] = -degree * node_count / 4.0
    derivative[-1, -1] = degree * node_count / 4.0
    return (derivative, weights)


DERIVATIVE, NODE_WEIGHTS = gll_tables()
DERIVATIVE = np.asarray(DERIVATIVE, np.float32)
WEIGHTS = [float(w) for w in np.asarray(4.0 * NODE_WEIGHTS, np.float32)]


def iota(shape, axis):
    return lax.broadcasted_iota(jnp.int32, shape, axis)


def one_hot(target, rows):
    return jnp.where(iota((rows, target.shape[1]), 0) == target, 1.0, 0.0).astype(BF16)


def mass_weight(i1, i2, i3):
    def at(index):
        value = jnp.full(index.shape, WEIGHTS[7], F32)
        for place in range(7):
            value = jnp.where(index == place, WEIGHTS[place], value)
        return value

    return at(i1) * at(i2) * at(i3)


def cube_row(block):
    lane = iota((1, 128), 1)
    return mass_weight((lane >> 6) + 2 * block, (lane >> 3) & 7, lane & 7)


def mm(a, b):
    return jnp.dot(a, b, preferred_element_type=F32)


def mm_t(a, b):
    return lax.dot_general(a, b, (((1,), (1,)), ((), ())), preferred_element_type=F32)


def split(x):
    high = x.astype(BF16)
    return high, (x - high.astype(F32)).astype(BF16)


def to_slabs():
    col = iota((1, ROWS), 1)
    snap = (col * 171) >> 11
    return one_hot((col - SLABS * snap) * SNAPS + snap, ROWS)


def face_table(around):
    col = iota((1, 128), 1)
    side = (col >> 6) * 7
    i1 = (col >> 3) & 7
    low = col & 7
    return one_hot(i1 * 64 + (side * 8 + low if around else low * 8 + side), NODES)


def edge_table():
    col = iota((1, 256), 1)
    i2 = col & 7
    row = jnp.where(i2 == 7, 128, 0) + (col & 120) + 7 * (col >> 7)
    return one_hot(jnp.where((i2 == 0) | (i2 == 7), row, -1), 256)


def swap_halves(x):
    return pltpu.roll(x, 64, 1)


def radial_table(base):
    same = (iota((64, NODES), 1) & 63) == iota((64, NODES), 0)
    return jnp.concatenate(
        [jnp.where(same, base[j : j + 1, :], 0.0) for j in range(8)], axis=0
    ).astype(BF16)


def inner_tables(base2, base3):
    lane = iota((8, 128), 1)
    diagonal = (lane & 7) == iota((8, 128), 0)
    tiles = []
    for g in range(16):
        along2 = jnp.where(diagonal & ((lane >> 6) == g // 8), base2[g % 8 : g % 8 + 1, :], 0.0)
        along3 = jnp.where((lane >> 3) == g, base3, 0.0)
        tiles.append(jnp.concatenate([along2, along3], axis=1))
    return jnp.concatenate(tiles, axis=0).astype(BF16)


def spectral_kernel(
    v_hbm, ext_hbm, const_hbm, w_ref, low_ref, high_ref, own_ref, v_ref, ext_ref, const_ref, sems
):
    copies = [
        pltpu.make_async_copy(source, target, sems.at[i])
        for i, (source, target) in enumerate(
            ((const_hbm, const_ref), (v_hbm, v_ref), (ext_hbm, ext_ref))
        )
    ]
    for copy in copies:
        copy.start()
    permutation = to_slabs()
    table = jnp.concatenate([face_table(False), face_table(True)], axis=1)
    copies[0].wait()
    base = const_ref[...]
    d1 = radial_table(base[:, :NODES])
    d23 = inner_tables(base[:, NODES : NODES + 128], base[:, NODES + 128 :])
    cubes = [cube_row(b) for b in range(4)]
    copies[1].wait()
    flat = v_ref[...].reshape(ROWS, NODES)
    field = mm(permutation, flat).astype(BF16)
    radial_part = mm(field[64:], d1)
    blocks = jnp.concatenate([field[:, 128 * b : 128 * b + 128] for b in range(4)], axis=0)
    other_part = mm(blocks, d23)
    copies[2].wait()
    lower = iota((SNAPS, 128), 1) < 64
    row8 = iota((8, 128), 0)
    volumes = jnp.zeros((8, 128), F32)
    tiles = {}
    for e in range(RADIAL):
        volume = ext_ref[0, 0, e] * ext_ref[1, 0, e] * ext_ref[2, 0, e]
        volumes = jnp.where(row8 == e, volume, volumes)
        s0, s1, s2 = (2.0 / jnp.full((1, 128), ext_ref[k, 0, e], F32) for k in range(3))
        for b in range(4):
            lanes = slice(128 * b, 128 * b + 128)
            mass = volume * cubes[b]

            def other(c, direction):
                at = ROWS * b + 64 * c + SNAPS * e
                return other_part[at : at + SNAPS, 128 * direction - 128 : 128 * direction]

            def radial(c):
                at = 64 * (c - 1) + SNAPS * e
                return radial_part[at : at + SNAPS, lanes]

            tiles[0, e, b] = mass * (s1 * other(2, 1) - s2 * other(1, 2))
            tiles[1, e, b] = mass * (s2 * other(0, 2) - s0 * radial(2))
            tiles[2, e, b] = mass * (s0 * radial(1) - s1 * other(0, 1))
    for c in range(3):
        inner = [tiles[c, e, 0] for e in range(RADIAL)]
        outer = [tiles[c, e, 3] for e in range(RADIAL)]
        for e in range(RADIAL - 1):
            tiles[c, e + 1, 0] += jnp.where(lower, swap_halves(outer[e]), 0.0)
            tiles[c, e, 3] += jnp.where(lower, 0.0, swap_halves(inner[e + 1]))
    whole = jnp.concatenate(
        [
            jnp.concatenate([tiles[c, e, b] for b in range(4)], axis=1)
            for c in range(3)
            for e in range(RADIAL)
        ],
        axis=0,
    )
    w_ref[...] = whole
    high, low = split(whole)
    faces = mm(high, table) + mm(low, table)
    for pair in range(SLABS // 2):
        at = 2 * SNAPS * pair
        rows = slice(SNAPS * pair, SNAPS * pair + SNAPS)
        for first, last, lo_ref, hi_ref in (
            (0, 128, own_ref.at[rows, 0:128], own_ref.at[rows, 128:256]),
            (128, 256, low_ref.at[rows, :], high_ref.at[rows, :]),
        ):
            even = faces[at : at + SNAPS, first:last]
            odd = faces[at + SNAPS : at + 2 * SNAPS, first:last]
            lo_ref[...] = jnp.where(lower, even, swap_halves(odd))
            hi_ref[...] = jnp.where(lower, swap_halves(even), odd)
    low_ref[HALF:Z_ROWS, :] = volumes
    high_ref[HALF:Z_ROWS, :] = volumes


def edge_kernel(left_ref, right_ref, mine_ref, own_ref, low_ref, high_ref):
    got = jnp.concatenate([left_ref[:HALF, :], right_ref[:HALF, :]], axis=1)
    high, low = split(got)
    table = edge_table()
    faces = own_ref[...] + mm(high, table) + mm(low, table)
    for lanes, out_ref in ((slice(0, 128), low_ref), (slice(128, 256), high_ref)):
        out_ref[:HALF, :] = faces[:, lanes]
        out_ref[HALF : HALF + 8, :] = mine_ref[HALF:, :]
        out_ref[HALF + 8 : HALF + 16, :] = left_ref[HALF:, :]
        out_ref[HALF + 16 :, :] = right_ref[HALF:, :]


def fold_table(rows):
    lane = iota((rows, 128), 1) & 15
    return jnp.where(lane == (iota((rows, 128), 0) & 15), 1.0, 0.0)


def own_lanes():
    return (iota((SNAPS, 128), 1) >> 4) == (iota((SNAPS, 128), 0) & 7)


def unpack(low_ref, high_ref):
    lower = iota((SNAPS, 128), 1) < 64
    got = []
    for pair in range(SLABS // 2):
        rows = slice(SNAPS * pair, SNAPS * pair + SNAPS)
        low, high = low_ref[rows, :], high_ref[rows, :]
        got += [
            jnp.where(lower, low, swap_halves(high)),
            jnp.where(lower, swap_halves(low), high),
        ]
    return jnp.concatenate(got, axis=0)


def spread_faces(low_ref, high_ref, around):
    high, low = split(unpack(low_ref, high_ref))
    table = face_table(around)
    return mm_t(high, table) + mm_t(low, table)


def ends(index, centre, first, last):
    return centre + jnp.where(index == 0, first, 0.0) + jnp.where(index == 7, last, 0.0)


def column(ref, i2):
    return ends(
        i2,
        ref[HALF : HALF + 8, :],
        ref[HALF + 8 : HALF + 16, :],
        ref[HALF + 16 : HALF + 24, :],
    )


def node_scale(mine, share):
    lane = iota((8, 128), 1)
    inner = jnp.where(lane < 64, pltpu.roll(share, 1, 0), 0.0)
    outer = jnp.where(lane < 64, 0.0, pltpu.roll(share, 7, 0))
    used = iota((8, 128), 0) < RADIAL
    scaled = []
    for b in range(4):
        cube = cube_row(b)
        around = share + (inner if b == 0 else outer if b == 3 else 0.0)
        total_mass = jnp.where(used, cube * around, 1.0)
        scaled.append(jnp.sqrt(mine * cube) / total_mass)
    return jnp.concatenate(scaled, axis=1)


def inner_kernel(w_ref, left_ref, right_ref, mine_ref, t_ref, g_ref):
    total = w_ref[...] + spread_faces(left_ref, right_ref, True)
    t_ref[...] = total
    lane = iota((8, 128), 1)
    mine = mine_ref[HALF:, :]
    share = ends((lane >> 3) & 7, mine, left_ref[HALF:, :], right_ref[HALF:, :])
    i3 = iota((8, NODES), 1) & 7
    scale = jnp.where((i3 == 0) | (i3 == 7), 0.0, node_scale(mine, share))
    stacked = []
    for slab in range(SLABS):
        e = slab % RADIAL
        rows = slice(SNAPS * slab, SNAPS * slab + SNAPS)
        stacked.append(jnp.concatenate(split(total[rows, :] * scale[e : e + 1, :]), axis=0))
    stacked = jnp.concatenate(stacked, axis=1)
    g_ref[...] = mm_t(stacked, stacked)


def gram_kernel(low_ref, before_ref, inner_ref, mine_ref, g_ref):
    lane = iota((8, 128), 1)
    row = iota((8, 128), 0)
    i1, i2 = (lane >> 3) & 7, lane & 7
    cube = mass_weight(i1[:1], i2[:1], jnp.zeros((1, 128), jnp.int32))
    both = mine_ref[HALF:, :] + before_ref[HALF : HALF + 8, :]
    share = column(low_ref, i2) + column(before_ref, i2)
    share = ends(i1, share, pltpu.roll(share, 1, 0), pltpu.roll(share, 7, 0))
    scale = jnp.sqrt(both * cube) / jnp.where(row < RADIAL, cube * share, 1.0)
    lower = iota((1, 128), 1) < 64
    stacked = []
    for pair in range(SLABS // 2):
        e = 2 * (pair % (RADIAL // 2))
        rows = slice(SNAPS * pair, SNAPS * pair + SNAPS)
        factor = jnp.where(lower, scale[e : e + 1, :], scale[e + 1 : e + 2, :])
        value = (low_ref[rows, :] + before_ref[rows, :]) * factor
        stacked.append(jnp.concatenate(split(value), axis=0))
    stacked = jnp.concatenate(stacked, axis=1)
    gram = inner_ref[...] + mm_t(stacked, stacked)
    spread = jnp.dot(gram, fold_table(2 * SNAPS), precision=lax.Precision.HIGHEST)
    spread = jnp.where(own_lanes(), spread[:SNAPS, :] + spread[SNAPS:, :], 0.0)
    packed = jnp.concatenate(
        [
            jnp.sum(spread[:8, :], axis=0, keepdims=True),
            jnp.sum(spread[8:, :], axis=0, keepdims=True),
        ],
        axis=0,
    )
    g_ref[...] = jnp.broadcast_to(packed[None], g_ref.shape)


def weighted(t_ref, before_ref, after_ref, left_ref, right_ref, mine_ref):
    total = t_ref[...] + spread_faces(before_ref, after_ref, False)
    lane = iota((8, 128), 1)
    i3, i2 = lane & 7, (lane >> 3) & 7
    mine = mine_ref[HALF:, :]
    share = ends(
        i3,
        ends(i2, mine, left_ref[HALF:, :], right_ref[HALF:, :]),
        column(before_ref, i2),
        column(after_ref, i2),
    )
    scale = node_scale(mine, share)
    pairs = []
    for slab in range(SLABS):
        e = slab % RADIAL
        rows = slice(SNAPS * slab, SNAPS * slab + SNAPS)
        pairs.append(split(total[rows, :] * scale[e : e + 1, :]))
    return pairs


def basis_kernel(row_count, g_ref, *refs):
    q_ref, r_ref, d_ref = refs[6:]
    pairs = weighted(*refs[:6])
    packed = jnp.sum(g_ref[...], axis=0)
    row = iota((SNAPS, 128), 0)
    lane = iota((SNAPS, 128), 1)
    spread = jnp.where(row < 8, packed[0:1, :], packed[1:2, :])
    spread = jnp.where(own_lanes(), spread, 0.0)
    target = iota((128, 128), 0)
    unfold = jnp.where((iota((128, 128), 1) & 15) == target, 1.0, 0.0)
    work = lax.dot_general(
        spread, unfold, (((1,), (1,)), ((), ())), precision=lax.Precision.HIGHEST
    )
    work = jnp.where(lane == row + SNAPS, 1.0, work)
    for k in range(SNAPS):
        pivot = lax.rsqrt(work[k : k + 1, k : k + 1])
        top = work[k : k + 1, :] * pivot
        left = work[:, k : k + 1] * pivot
        work = jnp.where(row > k, work - left * top, jnp.where(row == k, top, work))
    upper = jnp.where((lane >= row) & (lane < SNAPS), work, 0.0)
    inverse = pltpu.roll(work, 128 - SNAPS, 1)
    inverse = jnp.where(lane <= row, inverse, 0.0)
    r_ref[...] = upper[:, :SNAPS] * (1.0 / math.sqrt(row_count))
    shifted = pltpu.roll(upper, 127, 1)
    d_ref[...] = lax.dot_general(
        shifted, inverse, (((1,), (1,)), ((), ())), precision=lax.Precision.HIGHEST
    )[:, : SNAPS - 1]
    high, low = split(inverse[:, :SNAPS] * math.sqrt(row_count))
    left = jnp.concatenate([high, high, low], axis=1)
    rows = []
    for zh, zl in pairs:
        rows.append(mm(left, jnp.concatenate([zh, zl, zh], axis=0)).astype(BF16))
    basis = lax.dot_general(
        to_slabs(),
        jnp.concatenate(rows, axis=0),
        (((0,), (0,)), ((), ())),
        preferred_element_type=F32,
    ).astype(BF16)
    q_ref[...] = basis.reshape(q_ref.shape)


def call(kernel, out_shapes, args, hbm=(), scratch=()):
    vmem = pl.BlockSpec(memory_space=pltpu.VMEM)
    in_specs = [pl.BlockSpec(memory_space=pltpu.HBM) if i in hbm else vmem for i in range(len(args))]
    return pl.pallas_call(
        kernel,
        out_shape=[jax.ShapeDtypeStruct(shape, dtype) for shape, dtype in out_shapes],
        in_specs=in_specs,
        out_specs=[vmem] * len(out_shapes),
        scratch_shapes=list(scratch),
        compiler_params=pltpu.CompilerParams(vmem_limit_bytes=VMEM_BYTES),
    )(*[pltpu.with_memory_space_constraint(a, pltpu.HBM) if i in hbm else a for i, a in enumerate(args)])


def pass_on(x, axis, step):
    count = lax.axis_size(axis)
    return lax.ppermute(x, axis, [(i, (i + step) % count) for i in range(count)])


def from_everyone(copies, axis):
    return lax.all_to_all(copies, axis, split_axis=0, concat_axis=0, tiled=True)


def steps(velocity, extents):
    j, n = np.arange(8)[:, None], np.arange(NODES)[None, :]
    const = np.concatenate(
        [DERIVATIVE[n >> 6, j], DERIVATIVE[(n[:, :128] >> 3) & 7, j], DERIVATIVE[n[:, :128] & 7, j]],
        axis=1,
    )
    const = jnp.asarray(const)
    near, far = lax.axis_size(NEAR), lax.axis_size(FAR)
    row_count = 3 * RADIAL * NODES * lax.axis_size(WIDE) * lax.axis_size(NARROW)
    whole, low, high, own = call(
        spectral_kernel,
        [((ROWS, NODES), F32), ((Z_ROWS, 128), F32), ((Z_ROWS, 128), F32), ((HALF, 256), F32)],
        [velocity.reshape(SNAPS, 3, RADIAL, NODES), extents.reshape(3, 1, RADIAL), const],
        hbm=(0, 1, 2),
        scratch=[
            pltpu.VMEM((SNAPS, 3, RADIAL, NODES), BF16),
            pltpu.SMEM((3, 1, RADIAL), F32),
            pltpu.VMEM(const.shape, F32),
            pltpu.SemaphoreType.DMA((3,)),
        ],
    )
    left = pass_on(high, NARROW, 1)
    right = pass_on(low, NARROW, -1)
    z_low, z_high = call(edge_kernel, [((Y_ROWS, 128), F32)] * 2, [left, right, low, own])
    before = pass_on(z_high, WIDE, 1)
    after = pass_on(z_low, WIDE, -1)
    total, inner_gram = call(
        inner_kernel,
        [((ROWS, NODES), F32), ((2 * SNAPS, 2 * SNAPS), F32)],
        [whole, left, right, low],
    )
    gram = call(gram_kernel, [((near, 2, 128), F32)], [z_low, before, inner_gram, low])[0]
    gram = from_everyone(gram, NEAR)
    gram, after = lax.optimization_barrier((gram.sum(axis=0), after))
    gram = from_everyone(jnp.broadcast_to(gram, (far, 2, 128)), FAR)
    q_basis, r_factor, dmd_operator = call(
        functools.partial(basis_kernel, row_count),
        [
            ((SNAPS, 3, RADIAL, NODES), BF16),
            ((SNAPS, SNAPS), F32),
            ((SNAPS, SNAPS - 1), F32),
        ],
        [gram, total, before, after, left, right, low],
    )
    return (q_basis.reshape(velocity.shape), r_factor, dmd_operator)


def solution(mesh):
    sizes = tuple(mesh.shape.values())
    wide_0 = 4 if sizes[0] % 16 == 0 else 2
    narrow_1 = 2
    finer = Mesh(
        mesh.devices.reshape(wide_0, sizes[0] // wide_0, sizes[1] // narrow_1, narrow_1),
        (*WIDE, *NARROW),
    )
    placed = (P(None, None, WIDE, NARROW, None, None), P(None, WIDE, NARROW, None))
    return jax.shard_map(
        steps,
        mesh=finer,
        in_specs=placed,
        out_specs=(P(None, None, WIDE, NARROW, None, None), P(), P()),
        check_vma=False,
    )
```

profile of v0, /device:TPU:1, one launch (start us, length us, event | category | flops | bytes accessed | tf_op | source)
XLA Modules:
  0.0 59.7 jit_solution(438065183718305656)
XLA Ops:
  0.6 2.1 %shard_map.58 = (f32[192,512]{1,0:T(8,128)S(1)}, f32[104,128]{1,0:T(8,128)S(1)}, f32[104,128]{1,0:T(8,128)S(1)}, f32[96,256]{1,0:T(8,128)S(1)}) custom-call(bf16[16,3,4,512]{3,2,1,0:T(4,128)(2,1)} %bitcast.5, f32[3,1,4]{2,1,0:T(1,128)} %bitcast.6, f32[8,768]{1,0:T(8,128)} %constant.4.clone.const_hbm), custom_call_target="tpu_custom_call" | custom-call | tf_op jit(solution)/shard_map/pallas_call | solution.py:410
  2.7 2.7 %collective-permute-start = (f32[104,128]{1,0:T(8,128)S(1)}, f32[104,128]{1,0:T(8,128)S(1)}, u32[]{:S(2)}, u32[]{:S(2)}) collective-permute-start(f32[104,128]{1,0:T(8,128)S(1)} %get-tuple-element.16), channel_id=1, source_target_pairs={{0,1},{1,2},{2,3},{3,4},{4,5},{5,6},{6,7},{7,0},{8,9},{9,10},{10,1... | collective-permute-start | bytes 159752 | tf_op jit(solution)/shard_map/ppermute | solution.py:422
  5.4 4.2 %collective-permute-start.1 = (f32[104,128]{1,0:T(8,128)S(1)}, f32[104,128]{1,0:T(8,128)S(1)}, u32[]{:S(2)}, u32[]{:S(2)}) collective-permute-start(f32[104,128]{1,0:T(8,128)S(1)} %get-tuple-element.17.mine_ref.refs_5_), channel_id=1, source_target_pairs={{0,7},{1,0},{2,1},{3,2},{4,3},{5,4},{6,5},{7,6},{8,15},{9,8},{10,9... | collective-permute-start | bytes 159752 | tf_op jit(solution)/shard_map/ppermute | solution.py:422
  9.6 0.7 %collective-permute-done.left_ref.refs_3_ = f32[104,128]{1,0:T(8,128)S(1)} collective-permute-done((f32[104,128]{1,0:T(8,128)S(1)}, f32[104,128]{1,0:T(8,128)S(1)}, u32[]{:S(2)}, u32[]{:S(2)}) %collective-permute-start) | collective-permute-done | bytes 53280 | tf_op jit(solution)/shard_map/ppermute | solution.py:422
  10.3 0.2 collective-permute-done.1.right_ref.refs_4_
  10.5 0.2 shard_map.59
  10.7 2.0 %collective-permute-start.2 = (f32[120,128]{1,0:T(8,128)S(1)}, f32[120,128]{1,0:T(8,128)S(1)}, u32[]{:S(2)}, u32[]{:S(2)}) collective-permute-start(f32[120,128]{1,0:T(8,128)S(1)} %get-tuple-element.20), channel_id=1, source_target_pairs={{0,8},{8,16},{16,24},{24,32},{32,40},{40,48},{48,56},{56,64},{64,7... | collective-permute-start | bytes 184328 | tf_op jit(solution)/shard_map/ppermute | solution.py:422
  12.7 11.7 %collective-permute-start.3 = (f32[120,128]{1,0:T(8,128)S(1)}, f32[120,128]{1,0:T(8,128)S(1)}, u32[]{:S(2)}, u32[]{:S(2)}) collective-permute-start(f32[120,128]{1,0:T(8,128)S(1)} %get-tuple-element.19.low_ref), channel_id=1, source_target_pairs={{0,504},{8,0},{16,8},{24,16},{32,24},{40,32},{48,40},{56,48},{64,5... | collective-permute-start | bytes 184328 | tf_op jit(solution)/shard_map/ppermute | solution.py:422
  24.4 0.7 %shard_map.60 = (f32[192,512]{1,0:T(8,128)S(1)}, f32[32,32]{1,0:T(8,128)S(1)}) custom-call(f32[192,512]{1,0:T(8,128)S(1)} %get-tuple-element.21.w_ref, f32[104,128]{1,0:T(8,128)S(1)} %collective-permute-done.left_ref.refs_3_, f32[104,128]{1,0:T(8,128)S(1)} %collective-permute-done.1.right_ref.refs_4_, f32[104,128]{1,0:T(8,128)S(1)} %get-tuple-element.17.mine_ref.refs_5_), custom_call_target="tpu_custom_call" | custom-call | tf_op jit(solution)/shard_map/pallas_call | solution.py:410
  25.1 0.0 collective-permute-done.2.before_ref.refs_1_
  25.1 0.4 shard_map.61
  25.5 11.8 %all_to_all.10 = f32[32,2,128]{2,1,0:T(2,128)S(1)} all-to-all(f32[32,2,128]{2,1,0:T(2,128)S(1)} %shard_map.61), channel_id=1, replica_groups=mesh['wide_0'=4,'wide_1'=16,'narrow_0'=4,'narrow_1'=2] {'wide_0','narrow..., dimensions={0} | all-to-all | bytes 65536 | tf_op jit(solution)/shard_map/all_to_all | solution.py:426
  37.3 0.0 collective-permute-done.3.refs_2_
  37.3 19.6 %all_to_all.11.g_ref = f32[16,2,128]{2,1,0:T(2,128)S(1)} all-to-all(f32[16,2,128]{2,1,0:T(2,128)S(1)} %broadcast_in_dim.3), channel_id=1, replica_groups=mesh['wide_0'=4,'wide_1'=16,'narrow_0'=4,'narrow_1'=2] {'wide_1'}, dimensions={0} | all-to-all | bytes 32768 | tf_op jit(solution)/shard_map/all_to_all | solution.py:426
  56.9 2.8 %shard_map.62 = (bf16[16,3,4,512]{3,2,1,0:T(4,128)(2,1)}, f32[16,16]{1,0:T(8,128)}, f32[16,15]{1,0:T(8,128)}) custom-call(f32[16,2,128]{2,1,0:T(2,128)S(1)} %all_to_all.11.g_ref, f32[192,512]{1,0:T(8,128)S(1)} %get-tuple-element.24.refs_0_, f32[120,128]{1,0:T(8,128)S(1)} %collective-permute-done.2.before_ref.refs_1_, ...), custom_call_target="tpu_custom_call" | custom-call | tf_op jit(solution)/shard_map/pallas_call | solution.py:410
  (2 shorter events, 0.0 us)
Async XLA Ops:
  2.7 7.6 %collective-permute-start = (f32[104,128]{1,0:T(8,128)S(1)}, f32[104,128]{1,0:T(8,128)S(1)}, u32[]{:S(2)}, u32[]{:S(2)}) collective-permute-start(f32[104,128]{1,0:T(8,128)S(1)} %get-tuple-element.16), channel_id=1, source_target_pairs={{0,1},{1,2},{2,3},{3,4},{4,5},{5,6},{6,7},{7,0},{8,9},{9,10},{10,1... | collective-permute-start | bytes 159752 | tf_op jit(solution)/shard_map/ppermute | solution.py:422
  5.4 5.1 %collective-permute-start.1 = (f32[104,128]{1,0:T(8,128)S(1)}, f32[104,128]{1,0:T(8,128)S(1)}, u32[]{:S(2)}, u32[]{:S(2)}) collective-permute-start(f32[104,128]{1,0:T(8,128)S(1)} %get-tuple-element.17.mine_ref.refs_5_), channel_id=1, source_target_pairs={{0,7},{1,0},{2,1},{3,2},{4,3},{5,4},{6,5},{7,6},{8,15},{9,8},{10,9... | collective-permute-start | bytes 159752 | tf_op jit(solution)/shard_map/ppermute | solution.py:422
  10.7 14.4 %collective-permute-start.2 = (f32[120,128]{1,0:T(8,128)S(1)}, f32[120,128]{1,0:T(8,128)S(1)}, u32[]{:S(2)}, u32[]{:S(2)}) collective-permute-start(f32[120,128]{1,0:T(8,128)S(1)} %get-tuple-element.20), channel_id=1, source_target_pairs={{0,8},{8,16},{16,24},{24,32},{32,40},{40,48},{48,56},{56,64},{64,7... | collective-permute-start | bytes 184328 | tf_op jit(solution)/shard_map/ppermute | solution.py:422
  12.7 24.6 %collective-permute-start.3 = (f32[120,128]{1,0:T(8,128)S(1)}, f32[120,128]{1,0:T(8,128)S(1)}, u32[]{:S(2)}, u32[]{:S(2)}) collective-permute-start(f32[120,128]{1,0:T(8,128)S(1)} %get-tuple-element.19.low_ref), channel_id=1, source_target_pairs={{0,504},{8,0},{16,8},{24,16},{32,24},{40,32},{48,40},{56,48},{64,5... | collective-permute-start | bytes 184328 | tf_op jit(solution)/shard_map/ppermute | solution.py:422
where the time goes:
time: 59.9 us; the launch traced here: 59.7 us
  blocking collectives  31.3 us (52%)
  starting transfers between devices  20.6 us (34%)
  Pallas kernels  6.13 us (10%)
  waiting for transfers between devices  0.89 us (1%)
  between operations  0.68 us (1%)
    all_to_all x2, blocking collectives, from_everyone(): return lax.all_to_all(copies, axis, split_axis=0, concat_axis=0, tiled=True)  31.3 us
    ppermute x4, starting transfers between devices, pass_on(): lax.ppermute(x, axis, [(i, (i + step) % count) for i in range(count)])  20.6 us
    pallas_call x5, Pallas kernels, call(): pl.pallas_call(kernel, out_shape=[jax.ShapeDtypeStruct(shape, dtype) for...  6.13 us
  transfers between devices with their start and end apart: 4, of which 2 were waited for; matrix products, arithmetic and copies ran while one was open for 0% of the time, Pallas kernels for 2%

commit v1 on v0

--- a/solution.py
+++ b/solution.py
@@ -148,8 +148,18 @@
     return jnp.concatenate(tiles, axis=0).astype(BF16)
 
 
+def pack(faces, low_ref, high_ref):
+    lower = iota((SNAPS, 128), 1) < 64
+    for pair in range(SLABS // 2):
+        at = 2 * SNAPS * pair
+        rows = slice(SNAPS * pair, SNAPS * pair + SNAPS)
+        even, odd = faces[at : at + SNAPS, :], faces[at + SNAPS : at + 2 * SNAPS, :]
+        low_ref[rows, :] = jnp.where(lower, even, swap_halves(odd))
+        high_ref[rows, :] = jnp.where(lower, swap_halves(even), odd)
+
+
 def spectral_kernel(
-    v_hbm, ext_hbm, const_hbm, w_ref, low_ref, high_ref, own_ref, v_ref, ext_ref, const_ref, sems
+    v_hbm, ext_hbm, const_hbm, w_ref, low_ref, high_ref, v_ref, ext_ref, const_ref, sems
 ):
     copies = [
         pltpu.make_async_copy(source, target, sems.at[i])
@@ -160,7 +170,7 @@
     for copy in copies:
         copy.start()
     permutation = to_slabs()
-    table = jnp.concatenate([face_table(False), face_table(True)], axis=1)
+    table = face_table(True)
     copies[0].wait()
     base = const_ref[...]
     d1 = radial_table(base[:, :NODES])
@@ -213,17 +223,7 @@
     w_ref[...] = whole
     high, low = split(whole)
     faces = mm(high, table) + mm(low, table)
-    for pair in range(SLABS // 2):
-        at = 2 * SNAPS * pair
-        rows = slice(SNAPS * pair, SNAPS * pair + SNAPS)
-        for first, last, lo_ref, hi_ref in (
-            (0, 128, own_ref.at[rows, 0:128], own_ref.at[rows, 128:256]),
-            (128, 256, low_ref.at[rows, :], high_ref.at[rows, :]),
-        ):
-            even = faces[at : at + SNAPS, first:last]
-            odd = faces[at + SNAPS : at + 2 * SNAPS, first:last]
-            lo_ref[...] = jnp.where(lower, even, swap_halves(odd))
-            hi_ref[...] = jnp.where(lower, swap_halves(even), odd)
+    pack(faces, low_ref, high_ref)
     low_ref[HALF:Z_ROWS, :] = volumes
     high_ref[HALF:Z_ROWS, :] = volumes
 
@@ -295,42 +295,60 @@
     return jnp.concatenate(scaled, axis=1)
 
 
-def inner_kernel(w_ref, left_ref, right_ref, mine_ref, t_ref, g_ref):
-    total = w_ref[...] + spread_faces(left_ref, right_ref, True)
-    t_ref[...] = total
-    lane = iota((8, 128), 1)
+def stack(values):
+    parts = [jnp.concatenate(split(value), axis=0) for value in values]
+    parts = jnp.concatenate(parts, axis=1)
+    return mm_t(parts, parts)
+
+
+def deep_kernel(w_ref, mine_ref, own_ref, g_ref):
+    whole = w_ref[...]
+    high, low = split(whole)
+    table = face_table(False)
+    pack(mm(high, table) + mm(low, table), own_ref.at[:, 0:128], own_ref.at[:, 128:256])
+    lane = iota((8, NODES), 1)
+    i3, i2 = lane & 7, (lane >> 3) & 7
     mine = mine_ref[HALF:, :]
-    share = ends((lane >> 3) & 7, mine, left_ref[HALF:, :], right_ref[HALF:, :])
-    i3 = iota((8, NODES), 1) & 7
-    scale = jnp.where((i3 == 0) | (i3 == 7), 0.0, node_scale(mine, share))
-    stacked = []
+    edge = (i3 == 0) | (i3 == 7) | (i2 == 0) | (i2 == 7)
+    scale = jnp.where(edge, 0.0, node_scale(mine, mine))
+    values = []
     for slab in range(SLABS):
         e = slab % RADIAL
-        rows = slice(SNAPS * slab, SNAPS * slab + SNAPS)
-        stacked.append(jnp.concatenate(split(total[rows, :] * scale[e : e + 1, :]), axis=0))
-    stacked = jnp.concatenate(stacked, axis=1)
-    g_ref[...] = mm_t(stacked, stacked)
-
-
-def gram_kernel(low_ref, before_ref, inner_ref, mine_ref, g_ref):
+        values.append(whole[SNAPS * slab : SNAPS * slab + SNAPS, :] * scale[e : e + 1, :])
+    g_ref[...] = stack(values)
+
+
+def face_values(low_ref, other_ref, both, share, used):
     lane = iota((8, 128), 1)
-    row = iota((8, 128), 0)
-    i1, i2 = (lane >> 3) & 7, lane & 7
-    cube = mass_weight(i1[:1], i2[:1], jnp.zeros((1, 128), jnp.int32))
-    both = mine_ref[HALF:, :] + before_ref[HALF : HALF + 8, :]
-    share = column(low_ref, i2) + column(before_ref, i2)
+    i1, index = (lane >> 3) & 7, lane & 7
+    cube = mass_weight(i1[:1], index[:1], jnp.zeros((1, 128), jnp.int32))
     share = ends(i1, share, pltpu.roll(share, 1, 0), pltpu.roll(share, 7, 0))
-    scale = jnp.sqrt(both * cube) / jnp.where(row < RADIAL, cube * share, 1.0)
+    used = used & (iota((8, 128), 0) < RADIAL)
+    scale = jnp.where(used, jnp.sqrt(both * cube) / jnp.where(used, cube * share, 1.0), 0.0)
     lower = iota((1, 128), 1) < 64
-    stacked = []
+    values = []
     for pair in range(SLABS // 2):
         e = 2 * (pair % (RADIAL // 2))
         rows = slice(SNAPS * pair, SNAPS * pair + SNAPS)
         factor = jnp.where(lower, scale[e : e + 1, :], scale[e + 1 : e + 2, :])
-        value = (low_ref[rows, :] + before_ref[rows, :]) * factor
-        stacked.append(jnp.concatenate(split(value), axis=0))
-    stacked = jnp.concatenate(stacked, axis=1)
-    gram = inner_ref[...] + mm_t(stacked, stacked)
+        values.append((low_ref[rows, :] + other_ref[rows, :]) * factor)
+    return values
+
+
+def gram_kernel(z_low_ref, before_ref, y_low_ref, left_ref, inner_ref, g_ref):
+    index = iota((8, 128), 1) & 7
+    mine = y_low_ref[HALF:, :]
+    pair = mine + left_ref[HALF:, :]
+    inner = (index != 0) & (index != 7)
+    values = face_values(y_low_ref, left_ref, pair, pair, inner)
+    values += face_values(
+        z_low_ref,
+        before_ref,
+        mine + before_ref[HALF : HALF + 8, :],
+        column(z_low_ref, index) + column(before_ref, index),
+        index >= 0,
+    )
+    gram = inner_ref[...] + stack(values)
     spread = jnp.dot(gram, fold_table(2 * SNAPS), precision=lax.Precision.HIGHEST)
     spread = jnp.where(own_lanes(), spread[:SNAPS, :] + spread[SNAPS:, :], 0.0)
     packed = jnp.concatenate(
@@ -343,8 +361,12 @@
     g_ref[...] = jnp.broadcast_to(packed[None], g_ref.shape)
 
 
-def weighted(t_ref, before_ref, after_ref, left_ref, right_ref, mine_ref):
-    total = t_ref[...] + spread_faces(before_ref, after_ref, False)
+def weighted(w_ref, before_ref, after_ref, left_ref, right_ref, mine_ref):
+    total = (
+        w_ref[...]
+        + spread_faces(before_ref, after_ref, False)
+        + spread_faces(left_ref, right_ref, True)
+    )
     lane = iota((8, 128), 1)
     i3, i2 = lane & 7, (lane >> 3) & 7
     mine = mine_ref[HALF:, :]
@@ -377,11 +399,16 @@
         spread, unfold, (((1,), (1,)), ((), ())), precision=lax.Precision.HIGHEST
     )
     work = jnp.where(lane == row + SNAPS, 1.0, work)
-    for k in range(SNAPS):
-        pivot = lax.rsqrt(work[k : k + 1, k : k + 1])
-        top = work[k : k + 1, :] * pivot
-        left = work[:, k : k + 1] * pivot
-        work = jnp.where(row > k, work - left * top, jnp.where(row == k, top, work))
+    for first in range(0, SNAPS, 4):
+        block = range(first, first + 4)
+        lefts = [jnp.broadcast_to(work[:, k : k + 1], (SNAPS, 128)) for k in block]
+        for i, k in enumerate(block):
+            pivot = lax.rsqrt(lefts[i][k : k + 1, :])
+            left = lefts[i] * pivot
+            for j in range(i + 1, 4):
+                lefts[j] = lefts[j] - left * left[first + j : first + j + 1, :]
+            top = work[k : k + 1, :] * pivot
+            work = jnp.where(row > k, work - left * top, jnp.where(row == k, top, work))
     upper = jnp.where((lane >= row) & (lane < SNAPS), work, 0.0)
     inverse = pltpu.roll(work, 128 - SNAPS, 1)
     inverse = jnp.where(lane <= row, inverse, 0.0)
@@ -435,9 +462,9 @@
     const = jnp.asarray(const)
     near, far = lax.axis_size(NEAR), lax.axis_size(FAR)
     row_count = 3 * RADIAL * NODES * lax.axis_size(WIDE) * lax.axis_size(NARROW)
-    whole, low, high, own = call(
+    whole, low, high = call(
         spectral_kernel,
-        [((ROWS, NODES), F32), ((Z_ROWS, 128), F32), ((Z_ROWS, 128), F32), ((HALF, 256), F32)],
+        [((ROWS, NODES), F32), ((Z_ROWS, 128), F32), ((Z_ROWS, 128), F32)],
         [velocity.reshape(SNAPS, 3, RADIAL, NODES), extents.reshape(3, 1, RADIAL), const],
         hbm=(0, 1, 2),
         scratch=[
@@ -449,15 +476,13 @@
     )
     left = pass_on(high, NARROW, 1)
     right = pass_on(low, NARROW, -1)
+    own, inner_gram = call(
+        deep_kernel, [((HALF, 256), F32), ((2 * SNAPS, 2 * SNAPS), F32)], [whole, low]
+    )
     z_low, z_high = call(edge_kernel, [((Y_ROWS, 128), F32)] * 2, [left, right, low, own])
     before = pass_on(z_high, WIDE, 1)
     after = pass_on(z_low, WIDE, -1)
-    total, inner_gram = call(
-        inner_kernel,
-        [((ROWS, NODES), F32), ((2 * SNAPS, 2 * SNAPS), F32)],
-        [whole, left, right, low],
-    )
-    gram = call(gram_kernel, [((near, 2, 128), F32)], [z_low, before, inner_gram, low])[0]
+    gram = call(gram_kernel, [((near, 2, 128), F32)], [z_low, before, low, left, inner_gram])[0]
     gram = from_everyone(gram, NEAR)
     gram, after = lax.optimization_barrier((gram.sum(axis=0), after))
     gram = from_everyone(jnp.broadcast_to(gram, (far, 2, 128)), FAR)
@@ -468,7 +493,7 @@
             ((SNAPS, SNAPS), F32),
             ((SNAPS, SNAPS - 1), F32),
         ],
-        [gram, total, before, after, left, right, low],
+        [gram, whole, before, after, left, right, low],
     )
     return (q_basis.reshape(velocity.shape), r_factor, dmd_operator)
 

time: 59.9 us -> 58.6 us (0.978)
  Pallas kernels: 6.13 us -> 5.14 us
    pallas_call x5, Pallas kernels: 6.13 us -> 5.14 us  [call(): pl.pallas_call(kernel, out_shape=[jax.ShapeDtypeStruct(shape, dtype) for...]
  transfers between devices with their start and end apart: 4 -> 4, of which waited for: 2 -> 3; matrix products, arithmetic and copies ran while one was open for 0% -> 0% of each run, Pallas kernels for 2% -> 1%
where the time goes in v1:
time: 58.6 us; the launch traced here: 58.3 us
  blocking collectives  31 us (53%)
  starting transfers between devices  20.6 us (35%)
  Pallas kernels  5.14 us (9%)
  waiting for transfers between devices  0.87 us (1%)
  between operations  0.68 us (1%)
    all_to_all x2, blocking collectives, from_everyone(): return lax.all_to_all(copies, axis, split_axis=0, concat_axis=0, tiled=True)  31 us
    ppermute x4, starting transfers between devices, pass_on(): lax.ppermute(x, axis, [(i, (i + step) % count) for i in range(count)])  20.6 us
    pallas_call x5, Pallas kernels, call(): pl.pallas_call(kernel, out_shape=[jax.ShapeDtypeStruct(shape, dtype) for...  5.14 us
  transfers between devices with their start and end apart: 4, of which 3 were waited for; matrix products, arithmetic and copies ran while one was open for 0% of the time, Pallas kernels for 1%

profile of v1, /device:TPU:1, one launch (start us, length us, event | category | flops | bytes accessed | tf_op | source)
XLA Modules:
  0.0 58.3 jit_solution(13408351776324644344)
XLA Ops:
  0.6 2.1 %shard_map.58 = (f32[192,512]{1,0:T(8,128)S(1)}, f32[104,128]{1,0:T(8,128)S(1)}, f32[104,128]{1,0:T(8,128)S(1)}) custom-call(bf16[16,3,4,512]{3,2,1,0:T(4,128)(2,1)} %bitcast.5, f32[3,1,4]{2,1,0:T(1,128)} %bitcast.6, f32[8,768]{1,0:T(8,128)} %constant.4.clone.const_hbm), custom_call_target="tpu_custom_call" | custom-call | tf_op jit(solution)/shard_map/pallas_call | solution.py:437
  2.7 2.7 %collective-permute-start = (f32[104,128]{1,0:T(8,128)S(1)}, f32[104,128]{1,0:T(8,128)S(1)}, u32[]{:S(2)}, u32[]{:S(2)}) collective-permute-start(f32[104,128]{1,0:T(8,128)S(1)} %get-tuple-element.15), channel_id=1, source_target_pairs={{0,1},{1,2},{2,3},{3,4},{4,5},{5,6},{6,7},{7,0},{8,9},{9,10},{10,1... | collective-permute-start | bytes 159752 | tf_op jit(solution)/shard_map/ppermute | solution.py:449
  5.4 4.2 %collective-permute-start.1 = (f32[104,128]{1,0:T(8,128)S(1)}, f32[104,128]{1,0:T(8,128)S(1)}, u32[]{:S(2)}, u32[]{:S(2)}) collective-permute-start(f32[104,128]{1,0:T(8,128)S(1)} %get-tuple-element.16.mine_ref.y_low_ref.refs_5_), channel_id=1, source_target_pairs={{0,7},{1,0},{2,1},{3,2},{4,3},{5,4},{6,5},{7,6},{8,15},{9,8},{10,9... | collective-permute-start | bytes 159752 | tf_op jit(solution)/shard_map/ppermute | solution.py:449
  9.6 0.4 shard_map.59
  10.0 0.3 collective-permute-done.left_ref.refs_3_
  10.3 0.2 collective-permute-done.1.right_ref.refs_4_
  10.5 0.2 shard_map.60
  10.6 2.0 %collective-permute-start.2 = (f32[120,128]{1,0:T(8,128)S(1)}, f32[120,128]{1,0:T(8,128)S(1)}, u32[]{:S(2)}, u32[]{:S(2)}) collective-permute-start(f32[120,128]{1,0:T(8,128)S(1)} %get-tuple-element.20), channel_id=1, source_target_pairs={{0,8},{8,16},{16,24},{24,32},{32,40},{40,48},{48,56},{56,64},{64,7... | collective-permute-start | bytes 184328 | tf_op jit(solution)/shard_map/ppermute | solution.py:449
  12.7 11.7 %collective-permute-start.3 = (f32[120,128]{1,0:T(8,128)S(1)}, f32[120,128]{1,0:T(8,128)S(1)}, u32[]{:S(2)}, u32[]{:S(2)}) collective-permute-start(f32[120,128]{1,0:T(8,128)S(1)} %get-tuple-element.19.z_low_ref), channel_id=1, source_target_pairs={{0,504},{8,0},{16,8},{24,16},{32,24},{40,32},{48,40},{56,48},{64,5... | collective-permute-start | bytes 184328 | tf_op jit(solution)/shard_map/ppermute | solution.py:449
  24.4 0.4 collective-permute-done.2.before_ref.refs_1_
  24.8 0.4 shard_map.61
  25.2 11.4 %all_to_all.10 = f32[32,2,128]{2,1,0:T(2,128)S(1)} all-to-all(f32[32,2,128]{2,1,0:T(2,128)S(1)} %shard_map.61), channel_id=1, replica_groups=mesh['wide_0'=4,'wide_1'=16,'narrow_0'=4,'narrow_1'=2] {'wide_0','narrow..., dimensions={0} | all-to-all | bytes 65536 | tf_op jit(solution)/shard_map/all_to_all | solution.py:453
  36.6 0.0 collective-permute-done.3.refs_2_
  36.6 19.6 %all_to_all.11.g_ref = f32[16,2,128]{2,1,0:T(2,128)S(1)} all-to-all(f32[16,2,128]{2,1,0:T(2,128)S(1)} %broadcast_in_dim.3), channel_id=1, replica_groups=mesh['wide_0'=4,'wide_1'=16,'narrow_0'=4,'narrow_1'=2] {'wide_1'}, dimensions={0} | all-to-all | bytes 32768 | tf_op jit(solution)/shard_map/all_to_all | solution.py:453
  56.2 2.1 %shard_map.62 = (bf16[16,3,4,512]{3,2,1,0:T(4,128)(2,1)}, f32[16,16]{1,0:T(8,128)}, f32[16,15]{1,0:T(8,128)}) custom-call(f32[16,2,128]{2,1,0:T(2,128)S(1)} %all_to_all.11.g_ref, f32[192,512]{1,0:T(8,128)S(1)} %get-tuple-element.17.w_ref.refs_0_, f32[120,128]{1,0:T(8,128)S(1)} %collective-permute-done.2.before_ref.refs_1_, ...), custom_call_target="tpu_custom_call" | custom-call | tf_op jit(solution)/shard_map/pallas_call | solution.py:437
  (2 shorter events, 0.0 us)
Async XLA Ops:
  2.7 7.6 %collective-permute-start = (f32[104,128]{1,0:T(8,128)S(1)}, f32[104,128]{1,0:T(8,128)S(1)}, u32[]{:S(2)}, u32[]{:S(2)}) collective-permute-start(f32[104,128]{1,0:T(8,128)S(1)} %get-tuple-element.15), channel_id=1, source_target_pairs={{0,1},{1,2},{2,3},{3,4},{4,5},{5,6},{6,7},{7,0},{8,9},{9,10},{10,1... | collective-permute-start | bytes 159752 | tf_op jit(solution)/shard_map/ppermute | solution.py:449
  5.4 5.1 %collective-permute-start.1 = (f32[104,128]{1,0:T(8,128)S(1)}, f32[104,128]{1,0:T(8,128)S(1)}, u32[]{:S(2)}, u32[]{:S(2)}) collective-permute-start(f32[104,128]{1,0:T(8,128)S(1)} %get-tuple-element.16.mine_ref.y_low_ref.refs_5_), channel_id=1, source_target_pairs={{0,7},{1,0},{2,1},{3,2},{4,3},{5,4},{6,5},{7,6},{8,15},{9,8},{10,9... | collective-permute-start | bytes 159752 | tf_op jit(solution)/shard_map/ppermute | solution.py:449
  10.6 14.1 %collective-permute-start.2 = (f32[120,128]{1,0:T(8,128)S(1)}, f32[120,128]{1,0:T(8,128)S(1)}, u32[]{:S(2)}, u32[]{:S(2)}) collective-permute-start(f32[120,128]{1,0:T(8,128)S(1)} %get-tuple-element.20), channel_id=1, source_target_pairs={{0,8},{8,16},{16,24},{24,32},{32,40},{40,48},{48,56},{56,64},{64,7... | collective-permute-start | bytes 184328 | tf_op jit(solution)/shard_map/ppermute | solution.py:449
  12.7 23.9 %collective-permute-start.3 = (f32[120,128]{1,0:T(8,128)S(1)}, f32[120,128]{1,0:T(8,128)S(1)}, u32[]{:S(2)}, u32[]{:S(2)}) collective-permute-start(f32[120,128]{1,0:T(8,128)S(1)} %get-tuple-element.19.z_low_ref), channel_id=1, source_target_pairs={{0,504},{8,0},{16,8},{24,16},{32,24},{40,32},{48,40},{56,48},{64,5... | collective-permute-start | bytes 184328 | tf_op jit(solution)/shard_map/ppermute | solution.py:449

commit v2 on v1

--- a/solution.py
+++ b/solution.py
@@ -449,8 +449,12 @@
     return lax.ppermute(x, axis, [(i, (i + step) % count) for i in range(count)])
 
 
-def from_everyone(copies, axis):
-    return lax.all_to_all(copies, axis, split_axis=0, concat_axis=0, tiled=True)
+def from_everyone(copies, axis, first):
+    count = copies.shape[0]
+    order = [(first + i) % count for i in range(count)]
+    return lax.all_to_all(
+        copies, axis, split_axis=0, concat_axis=0, tiled=True, axis_index_groups=[order]
+    )
 
 
 def steps(velocity, extents):
@@ -483,9 +487,9 @@
     before = pass_on(z_high, WIDE, 1)
     after = pass_on(z_low, WIDE, -1)
     gram = call(gram_kernel, [((near, 2, 128), F32)], [z_low, before, low, left, inner_gram])[0]
-    gram = from_everyone(gram, NEAR)
+    gram = from_everyone(gram, NEAR, 2 * near // 3)
     gram, after = lax.optimization_barrier((gram.sum(axis=0), after))
-    gram = from_everyone(jnp.broadcast_to(gram, (far, 2, 128)), FAR)
+    gram = from_everyone(jnp.broadcast_to(gram, (far, 2, 128)), FAR, 9 * far // 16)
     q_basis, r_factor, dmd_operator = call(
         functools.partial(basis_kernel, row_count),
         [

time: 58.6 us -> 50.3 us (0.86)
  blocking collectives: 31 us -> 22.6 us
    all_to_all x2, blocking collectives: 31 us -> 22.6 us  [from_everyone(): lax.all_to_all(copies, axis, split_axis=0, concat_axis=0, tiled=True, axi...]
  transfers between devices with their start and end apart: 4 -> 4, of which waited for: 3 -> 3; matrix products, arithmetic and copies ran while one was open for 0% -> 0% of each run, Pallas kernels for 1% -> 2%
where the time goes in v2:
time: 50.3 us; the launch traced here: 49.9 us
  blocking collectives  22.6 us (45%)
  starting transfers between devices  20.6 us (41%)
  Pallas kernels  5.12 us (10%)
  waiting for transfers between devices  0.87 us (2%)
  between operations  0.68 us (1%)
    all_to_all x2, blocking collectives, from_everyone(): lax.all_to_all(copies, axis, split_axis=0, concat_axis=0, tiled=True, axi...  22.6 us
    ppermute x4, starting transfers between devices, pass_on(): lax.ppermute(x, axis, [(i, (i + step) % count) for i in range(count)])  20.6 us
    pallas_call x5, Pallas kernels, call(): pl.pallas_call(kernel, out_shape=[jax.ShapeDtypeStruct(shape, dtype) for...  5.12 us
  transfers between devices with their start and end apart: 4, of which 3 were waited for; matrix products, arithmetic and copies ran while one was open for 0% of the time, Pallas kernels for 2%

profile of v2, /device:TPU:1, one launch (start us, length us, event | category | flops | bytes accessed | tf_op | source)
XLA Modules:
  0.0 49.9 jit_solution(13000967518369076547)
XLA Ops:
  0.6 2.1 %shard_map.58 = (f32[192,512]{1,0:T(8,128)S(1)}, f32[104,128]{1,0:T(8,128)S(1)}, f32[104,128]{1,0:T(8,128)S(1)}) custom-call(bf16[16,3,4,512]{3,2,1,0:T(4,128)(2,1)} %bitcast.5, f32[3,1,4]{2,1,0:T(1,128)} %bitcast.6, f32[8,768]{1,0:T(8,128)} %constant.4.clone.const_hbm), custom_call_target="tpu_custom_call" | custom-call | tf_op jit(solution)/shard_map/pallas_call | solution.py:437
  2.7 2.7 %collective-permute-start = (f32[104,128]{1,0:T(8,128)S(1)}, f32[104,128]{1,0:T(8,128)S(1)}, u32[]{:S(2)}, u32[]{:S(2)}) collective-permute-start(f32[104,128]{1,0:T(8,128)S(1)} %get-tuple-element.15), channel_id=1, source_target_pairs={{0,1},{1,2},{2,3},{3,4},{4,5},{5,6},{6,7},{7,0},{8,9},{9,10},{10,1... | collective-permute-start | bytes 159752 | tf_op jit(solution)/shard_map/ppermute | solution.py:449
  5.4 4.2 %collective-permute-start.1 = (f32[104,128]{1,0:T(8,128)S(1)}, f32[104,128]{1,0:T(8,128)S(1)}, u32[]{:S(2)}, u32[]{:S(2)}) collective-permute-start(f32[104,128]{1,0:T(8,128)S(1)} %get-tuple-element.16.mine_ref.y_low_ref.refs_5_), channel_id=1, source_target_pairs={{0,7},{1,0},{2,1},{3,2},{4,3},{5,4},{6,5},{7,6},{8,15},{9,8},{10,9... | collective-permute-start | bytes 159752 | tf_op jit(solution)/shard_map/ppermute | solution.py:449
  9.6 0.4 shard_map.59
  10.0 0.3 collective-permute-done.left_ref.refs_3_
  10.3 0.2 collective-permute-done.1.right_ref.refs_4_
  10.5 0.2 shard_map.60
  10.6 2.0 %collective-permute-start.2 = (f32[120,128]{1,0:T(8,128)S(1)}, f32[120,128]{1,0:T(8,128)S(1)}, u32[]{:S(2)}, u32[]{:S(2)}) collective-permute-start(f32[120,128]{1,0:T(8,128)S(1)} %get-tuple-element.20), channel_id=1, source_target_pairs={{0,8},{8,16},{16,24},{24,32},{32,40},{40,48},{48,56},{56,64},{64,7... | collective-permute-start | bytes 184328 | tf_op jit(solution)/shard_map/ppermute | solution.py:449
  12.7 11.7 %collective-permute-start.3 = (f32[120,128]{1,0:T(8,128)S(1)}, f32[120,128]{1,0:T(8,128)S(1)}, u32[]{:S(2)}, u32[]{:S(2)}) collective-permute-start(f32[120,128]{1,0:T(8,128)S(1)} %get-tuple-element.19.z_low_ref), channel_id=1, source_target_pairs={{0,504},{8,0},{16,8},{24,16},{32,24},{40,32},{48,40},{56,48},{64,5... | collective-permute-start | bytes 184328 | tf_op jit(solution)/shard_map/ppermute | solution.py:449
  24.4 0.4 collective-permute-done.2.before_ref.refs_1_
  24.8 0.4 shard_map.61
  25.2 9.4 %all_to_all.10 = f32[32,2,128]{2,1,0:T(2,128)S(1)} all-to-all(f32[32,2,128]{2,1,0:T(2,128)S(1)} %shard_map.61), channel_id=1, replica_groups={{261,262,263,384,385,386,387,388,389,390,391,0,1,2,3,4,5,6,7,128,129,13..., dimensions={0} | all-to-all | bytes 65536 | tf_op jit(solution)/shard_map/all_to_all | solution.py:455
  34.6 0.0 collective-permute-done.3.refs_2_
  34.6 13.2 %all_to_all.11.g_ref = f32[16,2,128]{2,1,0:T(2,128)S(1)} all-to-all(f32[16,2,128]{2,1,0:T(2,128)S(1)} %broadcast_in_dim.3), channel_id=1, replica_groups={{72,80,88,96,104,112,120,0,8,16,24,32,40,48,56,64},{73,81,89,97,105,113..., dimensions={0} | all-to-all | bytes 32768 | tf_op jit(solution)/shard_map/all_to_all | solution.py:455
  47.8 2.1 %shard_map.62 = (bf16[16,3,4,512]{3,2,1,0:T(4,128)(2,1)}, f32[16,16]{1,0:T(8,128)}, f32[16,15]{1,0:T(8,128)}) custom-call(f32[16,2,128]{2,1,0:T(2,128)S(1)} %all_to_all.11.g_ref, f32[192,512]{1,0:T(8,128)S(1)} %get-tuple-element.17.w_ref.refs_0_, f32[120,128]{1,0:T(8,128)S(1)} %collective-permute-done.2.before_ref.refs_1_, ...), custom_call_target="tpu_custom_call" | custom-call | tf_op jit(solution)/shard_map/pallas_call | solution.py:437
  (2 shorter events, 0.0 us)
Async XLA Ops:
  2.7 7.6 %collective-permute-start = (f32[104,128]{1,0:T(8,128)S(1)}, f32[104,128]{1,0:T(8,128)S(1)}, u32[]{:S(2)}, u32[]{:S(2)}) collective-permute-start(f32[104,128]{1,0:T(8,128)S(1)} %get-tuple-element.15), channel_id=1, source_target_pairs={{0,1},{1,2},{2,3},{3,4},{4,5},{5,6},{6,7},{7,0},{8,9},{9,10},{10,1... | collective-permute-start | bytes 159752 | tf_op jit(solution)/shard_map/ppermute | solution.py:449
  5.4 5.1 %collective-permute-start.1 = (f32[104,128]{1,0:T(8,128)S(1)}, f32[104,128]{1,0:T(8,128)S(1)}, u32[]{:S(2)}, u32[]{:S(2)}) collective-permute-start(f32[104,128]{1,0:T(8,128)S(1)} %get-tuple-element.16.mine_ref.y_low_ref.refs_5_), channel_id=1, source_target_pairs={{0,7},{1,0},{2,1},{3,2},{4,3},{5,4},{6,5},{7,6},{8,15},{9,8},{10,9... | collective-permute-start | bytes 159752 | tf_op jit(solution)/shard_map/ppermute | solution.py:449
  10.6 14.1 %collective-permute-start.2 = (f32[120,128]{1,0:T(8,128)S(1)}, f32[120,128]{1,0:T(8,128)S(1)}, u32[]{:S(2)}, u32[]{:S(2)}) collective-permute-start(f32[120,128]{1,0:T(8,128)S(1)} %get-tuple-element.20), channel_id=1, source_target_pairs={{0,8},{8,16},{16,24},{24,32},{32,40},{40,48},{48,56},{56,64},{64,7... | collective-permute-start | bytes 184328 | tf_op jit(solution)/shard_map/ppermute | solution.py:449
  12.7 21.9 %collective-permute-start.3 = (f32[120,128]{1,0:T(8,128)S(1)}, f32[120,128]{1,0:T(8,128)S(1)}, u32[]{:S(2)}, u32[]{:S(2)}) collective-permute-start(f32[120,128]{1,0:T(8,128)S(1)} %get-tuple-element.19.z_low_ref), channel_id=1, source_target_pairs={{0,504},{8,0},{16,8},{24,16},{32,24},{40,32},{48,40},{56,48},{64,5... | collective-permute-start | bytes 184328 | tf_op jit(solution)/shard_map/ppermute | solution.py:449

commit v3 on v2

--- a/solution.py
+++ b/solution.py
@@ -24,8 +24,8 @@
 NODES = 512
 HALF = ROWS // 2
 Z_ROWS = HALF + 8
-Y_ROWS = HALF + 24
 VMEM_BYTES = 16 << 20
+CHUNKS = 2
 
 
 def gll_tables():
@@ -111,6 +111,11 @@
     return one_hot((col - SLABS * snap) * SNAPS + snap, ROWS)
 
 
+def from_slabs():
+    col = iota((1, ROWS), 1)
+    return one_hot((col & 15) * SLABS + (col >> 4), ROWS)
+
+
 def face_table(around):
     col = iota((1, 128), 1)
     side = (col >> 6) * 7
@@ -158,8 +163,23 @@
         high_ref[rows, :] = jnp.where(lower, swap_halves(even), odd)
 
 
+def face_derivatives(base1, base2, base3):
+    lane = iota((8, 128), 1)
+    side, i1, i3 = lane >> 6, (lane >> 3) & 7, lane & 7
+    third = i3 == iota((8, 128), 0)
+    zero = jnp.zeros((8, 128), F32)
+    first, second, last = [], [], []
+    for j1 in range(8):
+        for j2 in range(8):
+            end = None if 0 < j2 < 7 else side == j2 // 7
+            first.append(zero if end is None else jnp.where(third & end, base1[j1 : j1 + 1, :], 0.0))
+            second.append(jnp.where(third & (i1 == j1), base2[j2 : j2 + 1, :], 0.0))
+            last.append(zero if end is None else jnp.where(end & (i1 == j1), base3, 0.0))
+    return [jnp.concatenate(tiles, axis=0).astype(BF16) for tiles in (first, second, last)]
+
+
 def spectral_kernel(
-    v_hbm, ext_hbm, const_hbm, w_ref, low_ref, high_ref, v_ref, ext_ref, const_ref, sems
+    v_hbm, ext_hbm, const_hbm, field_ref, scale_ref, low_ref, high_ref, v_ref, ext_ref, const_ref, sems
 ):
     copies = [
         pltpu.make_async_copy(source, target, sems.at[i])
@@ -170,30 +190,72 @@
     for copy in copies:
         copy.start()
     permutation = to_slabs()
-    table = face_table(True)
+    lane = iota((1, 128), 1)
+    i1 = (lane >> 3) & 7
+    cube = mass_weight(i1, (lane >> 6) * 7, lane & 7)
     copies[0].wait()
-    base = const_ref[...]
-    d1 = radial_table(base[:, :NODES])
-    d23 = inner_tables(base[:, NODES : NODES + 128], base[:, NODES + 128 :])
-    cubes = [cube_row(b) for b in range(4)]
+    base = [const_ref[:, NODES + 128 * k : NODES + 128 * k + 128] for k in range(2, 5)]
+    d1, d2, d3 = face_derivatives(*base)
     copies[1].wait()
     flat = v_ref[...].reshape(ROWS, NODES)
     field = mm(permutation, flat).astype(BF16)
-    radial_part = mm(field[64:], d1)
-    blocks = jnp.concatenate([field[:, 128 * b : 128 * b + 128] for b in range(4)], axis=0)
-    other_part = mm(blocks, d23)
+    field_ref[...] = field
+    along1 = mm(field[64:], d1)
+    others = mm(field, jnp.concatenate([d2, d3], axis=1))
     copies[2].wait()
-    lower = iota((SNAPS, 128), 1) < 64
     row8 = iota((8, 128), 0)
     volumes = jnp.zeros((8, 128), F32)
-    tiles = {}
+    faces = {}
     for e in range(RADIAL):
         volume = ext_ref[0, 0, e] * ext_ref[1, 0, e] * ext_ref[2, 0, e]
         volumes = jnp.where(row8 == e, volume, volumes)
         s0, s1, s2 = (2.0 / jnp.full((1, 128), ext_ref[k, 0, e], F32) for k in range(3))
+        for k, scale in enumerate((s0, s1, s2)):
+            scale_ref[RADIAL * k + e : RADIAL * k + e + 1, :] = scale
+        mass = volume * cube
+
+        def other(c, direction):
+            at = 64 * c + SNAPS * e
+            return others[at : at + SNAPS, 128 * direction - 128 : 128 * direction]
+
+        def radial(c):
+            at = 64 * (c - 1) + SNAPS * e
+            return along1[at : at + SNAPS, :]
+
+        faces[0, e] = mass * (s1 * other(2, 1) - s2 * other(1, 2))
+        faces[1, e] = mass * (s2 * other(0, 2) - s0 * radial(2))
+        faces[2, e] = mass * (s0 * radial(1) - s1 * other(0, 1))
+    summed = []
+    for c in range(3):
+        for e in range(RADIAL):
+            face = faces[c, e]
+            if e > 0:
+                face = face + jnp.where(i1 == 0, pltpu.roll(faces[c, e - 1], 72, 1), 0.0)
+            if e < RADIAL - 1:
+                face = face + jnp.where(i1 == 7, pltpu.roll(faces[c, e + 1], 56, 1), 0.0)
+            summed.append(face)
+    pack(jnp.concatenate(summed, axis=0), low_ref, high_ref)
+    low_ref[HALF:Z_ROWS, :] = volumes
+    high_ref[HALF:Z_ROWS, :] = volumes
+
+
+def deep_kernel(field_ref, scale_ref, mine_ref, const_ref, w_ref, own_ref, g_ref):
+    base = const_ref[...]
+    d1 = radial_table(base[:, :NODES])
+    d23 = inner_tables(base[:, NODES : NODES + 128], base[:, NODES + 128 : NODES + 256])
+    field = field_ref[...]
+    radial_part = mm(field[64:], d1)
+    blocks = jnp.concatenate([field[:, 128 * b : 128 * b + 128] for b in range(4)], axis=0)
+    other_part = mm(blocks, d23)
+    lower = iota((SNAPS, 128), 1) < 64
+    mine = mine_ref[HALF:, :]
+    cubes = [cube_row(b) for b in range(4)]
+    tiles = {}
+    for e in range(RADIAL):
+        s0, s1, s2 = (scale_ref[RADIAL * k + e : RADIAL * k + e + 1, :] for k in range(3))
         for b in range(4):
             lanes = slice(128 * b, 128 * b + 128)
-            mass = volume * cubes[b]
+            mass = mine[e : e + 1, :] * cubes[b]
 
             def other(c, direction):
                 at = ROWS * b + 64 * c + SNAPS * e
@@ -212,20 +274,23 @@
         for e in range(RADIAL - 1):
             tiles[c, e + 1, 0] += jnp.where(lower, swap_halves(outer[e]), 0.0)
             tiles[c, e, 3] += jnp.where(lower, 0.0, swap_halves(inner[e + 1]))
-    whole = jnp.concatenate(
-        [
-            jnp.concatenate([tiles[c, e, b] for b in range(4)], axis=1)
-            for c in range(3)
-            for e in range(RADIAL)
-        ],
-        axis=0,
-    )
+    slabs = [
+        jnp.concatenate([tiles[c, e, b] for b in range(4)], axis=1)
+        for c in range(3)
+        for e in range(RADIAL)
+    ]
+    whole = jnp.concatenate(slabs, axis=0)
     w_ref[...] = whole
     high, low = split(whole)
-    faces = mm(high, table) + mm(low, table)
-    pack(faces, low_ref, high_ref)
-    low_ref[HALF:Z_ROWS, :] = volumes
-    high_ref[HALF:Z_ROWS, :] = volumes
+    table = face_table(False)
+    pack(mm(high, table) + mm(low, table), own_ref.at[:, 0:128], own_ref.at[:, 128:256])
+    lane = iota((8, NODES), 1)
+    i3, i2 = lane & 7, (lane >> 3) & 7
+    edge = (i3 == 0) | (i3 == 7) | (i2 == 0) | (i2 == 7)
+    scale = jnp.where(edge, 0.0, node_scale(mine, mine))
+    g_ref[...] = stack(
+        [slab * scale[i % RADIAL : i % RADIAL + 1, :] for i, slab in enumerate(slabs)]
+    )
 
 
 def edge_kernel(left_ref, right_ref, mine_ref, own_ref, low_ref, high_ref):
@@ -233,20 +298,14 @@
     high, low = split(got)
     table = edge_table()
     faces = own_ref[...] + mm(high, table) + mm(low, table)
+    lower = iota((8, 128), 1) < 64
+    volumes = jnp.where(lower, mine_ref[HALF:, :], left_ref[HALF:, :])
+    volumes = jnp.where(
+        iota((8, 128), 0) < RADIAL, volumes, pltpu.roll(right_ref[HALF:, :], RADIAL, 0)
+    )
     for lanes, out_ref in ((slice(0, 128), low_ref), (slice(128, 256), high_ref)):
         out_ref[:HALF, :] = faces[:, lanes]
-        out_ref[HALF : HALF + 8, :] = mine_ref[HALF:, :]
-        out_ref[HALF + 8 : HALF + 16, :] = left_ref[HALF:, :]
-        out_ref[HALF + 16 :, :] = right_ref[HALF:, :]
-
-
-def fold_table(rows):
-    lane = iota((rows, 128), 1) & 15
-    return jnp.where(lane == (iota((rows, 128), 0) & 15), 1.0, 0.0)
-
-
-def own_lanes():
-    return (iota((SNAPS, 128), 1) >> 4) == (iota((SNAPS, 128), 0) & 7)
+        out_ref[HALF:, :] = volumes
 
 
 def unpack(low_ref, high_ref):
@@ -272,13 +331,20 @@
     return centre + jnp.where(index == 0, first, 0.0) + jnp.where(index == 7, last, 0.0)
 
 
+def volumes_of(ref):
+    sent = ref[HALF:, :]
+    lower = iota((8, 128), 1) < 64
+    swapped = swap_halves(sent)
+    triple = (
+        jnp.where(lower, sent, swapped),
+        jnp.where(lower, swapped, sent),
+        pltpu.roll(sent, RADIAL, 0),
+    )
+    return [jnp.where(iota((8, 128), 0) < RADIAL, volume, 0.0) for volume in triple]
+
+
 def column(ref, i2):
-    return ends(
-        i2,
-        ref[HALF : HALF + 8, :],
-        ref[HALF + 8 : HALF + 16, :],
-        ref[HALF + 16 : HALF + 24, :],
-    )
+    return ends(i2, *volumes_of(ref))
 
 
 def node_scale(mine, share):
@@ -299,23 +365,6 @@
     parts = [jnp.concatenate(split(value), axis=0) for value in values]
     parts = jnp.concatenate(parts, axis=1)
     return mm_t(parts, parts)
-
-
-def deep_kernel(w_ref, mine_ref, own_ref, g_ref):
-    whole = w_ref[...]
-    high, low = split(whole)
-    table = face_table(False)
-    pack(mm(high, table) + mm(low, table), own_ref.at[:, 0:128], own_ref.at[:, 128:256])
-    lane = iota((8, NODES), 1)
-    i3, i2 = lane & 7, (lane >> 3) & 7
-    mine = mine_ref[HALF:, :]
-    edge = (i3 == 0) | (i3 == 7) | (i2 == 0) | (i2 == 7)
-    scale = jnp.where(edge, 0.0, node_scale(mine, mine))
-    values = []
-    for slab in range(SLABS):
-        e = slab % RADIAL
-        values.append(whole[SNAPS * slab : SNAPS * slab + SNAPS, :] * scale[e : e + 1, :])
-    g_ref[...] = stack(values)
 
 
 def face_values(low_ref, other_ref, both, share, used):
@@ -344,13 +393,16 @@
     values += face_values(
         z_low_ref,
         before_ref,
-        mine + before_ref[HALF : HALF + 8, :],
+        mine + volumes_of(before_ref)[0],
         column(z_low_ref, index) + column(before_ref, index),
         index >= 0,
     )
     gram = inner_ref[...] + stack(values)
-    spread = jnp.dot(gram, fold_table(2 * SNAPS), precision=lax.Precision.HIGHEST)
-    spread = jnp.where(own_lanes(), spread[:SNAPS, :] + spread[SNAPS:, :], 0.0)
+    gram = jnp.concatenate([gram, jnp.zeros((2 * SNAPS, 128 - 2 * SNAPS), F32)], axis=1)
+    gram = gram[:SNAPS, :] + gram[SNAPS:, :]
+    gram = gram + pltpu.roll(gram, 128 - SNAPS, 1)
+    gram = jnp.where(iota((SNAPS, 128), 1) < SNAPS, gram, 0.0)
+    spread = pltpu.roll(gram, 0, 1, stride=SNAPS, stride_axis=0)
     packed = jnp.concatenate(
         [
             jnp.sum(spread[:8, :], axis=0, keepdims=True),
@@ -386,26 +438,29 @@
 
 
 def basis_kernel(row_count, g_ref, *refs):
-    q_ref, r_ref, d_ref = refs[6:]
+    q_hbm, r_hbm, d_hbm, q_ref, r_ref, d_ref, sems = refs[6:]
+    copies = [
+        pltpu.make_async_copy(r_ref, r_hbm, sems.at[0]),
+        pltpu.make_async_copy(d_ref, d_hbm, sems.at[1]),
+    ]
     pairs = weighted(*refs[:6])
     packed = jnp.sum(g_ref[...], axis=0)
     row = iota((SNAPS, 128), 0)
     lane = iota((SNAPS, 128), 1)
     spread = jnp.where(row < 8, packed[0:1, :], packed[1:2, :])
-    spread = jnp.where(own_lanes(), spread, 0.0)
-    target = iota((128, 128), 0)
-    unfold = jnp.where((iota((128, 128), 1) & 15) == target, 1.0, 0.0)
-    work = lax.dot_general(
-        spread, unfold, (((1,), (1,)), ((), ())), precision=lax.Precision.HIGHEST
-    )
+    work = spread
+    for place in range(1, 8):
+        moved = pltpu.roll(spread, 128 - SNAPS * place, 1)
+        work = jnp.where((row & 7) == place, moved, work)
+    work = jnp.where(lane < SNAPS, work, 0.0)
     work = jnp.where(lane == row + SNAPS, 1.0, work)
-    for first in range(0, SNAPS, 4):
-        block = range(first, first + 4)
+    for first in range(0, SNAPS, 16):
+        block = range(first, first + 16)
         lefts = [jnp.broadcast_to(work[:, k : k + 1], (SNAPS, 128)) for k in block]
         for i, k in enumerate(block):
             pivot = lax.rsqrt(lefts[i][k : k + 1, :])
             left = lefts[i] * pivot
-            for j in range(i + 1, 4):
+            for j in range(i + 1, SNAPS):
                 lefts[j] = lefts[j] - left * left[first + j : first + j + 1, :]
             top = work[k : k + 1, :] * pivot
             work = jnp.where(row > k, work - left * top, jnp.where(row == k, top, work))
@@ -417,28 +472,35 @@
     d_ref[...] = lax.dot_general(
         shifted, inverse, (((1,), (1,)), ((), ())), precision=lax.Precision.HIGHEST
     )[:, : SNAPS - 1]
+    for copy in copies:
+        copy.start()
     high, low = split(inverse[:, :SNAPS] * math.sqrt(row_count))
     left = jnp.concatenate([high, high, low], axis=1)
     rows = []
     for zh, zl in pairs:
         rows.append(mm(left, jnp.concatenate([zh, zl, zh], axis=0)).astype(BF16))
-    basis = lax.dot_general(
-        to_slabs(),
-        jnp.concatenate(rows, axis=0),
-        (((0,), (0,)), ((), ())),
-        preferred_element_type=F32,
-    ).astype(BF16)
-    q_ref[...] = basis.reshape(q_ref.shape)
-
-
-def call(kernel, out_shapes, args, hbm=(), scratch=()):
+    rows = jnp.concatenate(rows, axis=0)
+    permutation = from_slabs()
+    for part in range(CHUNKS):
+        count = SNAPS // CHUNKS
+        snaps = slice(count * part, count * part + count)
+        chosen = permutation[SLABS * count * part : SLABS * count * (part + 1), :]
+        q_ref[snaps] = mm(chosen, rows).astype(BF16).reshape(count, 3, RADIAL, NODES)
+        copy = pltpu.make_async_copy(q_ref.at[snaps], q_hbm.at[snaps], sems.at[2 + part])
+        copy.start()
+        copies.append(copy)
+    for copy in copies:
+        copy.wait()
+
+
+def call(kernel, out_shapes, args, hbm=(), scratch=(), hbm_out=False):
     vmem = pl.BlockSpec(memory_space=pltpu.VMEM)
     in_specs = [pl.BlockSpec(memory_space=pltpu.HBM) if i in hbm else vmem for i in range(len(args))]
     return pl.pallas_call(
         kernel,
         out_shape=[jax.ShapeDtypeStruct(shape, dtype) for shape, dtype in out_shapes],
         in_specs=in_specs,
-        out_specs=[vmem] * len(out_shapes),
+        out_specs=[pl.BlockSpec(memory_space=pltpu.HBM) if hbm_out else vmem] * len(out_shapes),
         scratch_shapes=list(scratch),
         compiler_params=pltpu.CompilerParams(vmem_limit_bytes=VMEM_BYTES),
     )(*[pltpu.with_memory_space_constraint(a, pltpu.HBM) if i in hbm else a for i, a in enumerate(args)])
@@ -459,16 +521,20 @@
 
 def steps(velocity, extents):
     j, n = np.arange(8)[:, None], np.arange(NODES)[None, :]
-    const = np.concatenate(
-        [DERIVATIVE[n >> 6, j], DERIVATIVE[(n[:, :128] >> 3) & 7, j], DERIVATIVE[n[:, :128] & 7, j]],
-        axis=1,
-    )
-    const = jnp.asarray(const)
+    m = n[:, :128]
+    places = (n >> 6, (m >> 3) & 7, m & 7, (m >> 3) & 7, (m >> 6) * 7, m & 7)
+    const = jnp.asarray(np.concatenate([DERIVATIVE[place, j] for place in places], axis=1))
+
     near, far = lax.axis_size(NEAR), lax.axis_size(FAR)
     row_count = 3 * RADIAL * NODES * lax.axis_size(WIDE) * lax.axis_size(NARROW)
-    whole, low, high = call(
+    field, scales, low, high = call(
         spectral_kernel,
-        [((ROWS, NODES), F32), ((Z_ROWS, 128), F32), ((Z_ROWS, 128), F32)],
+        [
+            ((ROWS, NODES), BF16),
+            ((SNAPS, 128), F32),
+            ((Z_ROWS, 128), F32),
+            ((Z_ROWS, 128), F32),
+        ],
         [velocity.reshape(SNAPS, 3, RADIAL, NODES), extents.reshape(3, 1, RADIAL), const],
         hbm=(0, 1, 2),
         scratch=[
@@ -480,10 +546,12 @@
     )
     left = pass_on(high, NARROW, 1)
     right = pass_on(low, NARROW, -1)
-    own, inner_gram = call(
-        deep_kernel, [((HALF, 256), F32), ((2 * SNAPS, 2 * SNAPS), F32)], [whole, low]
-    )
-    z_low, z_high = call(edge_kernel, [((Y_ROWS, 128), F32)] * 2, [left, right, low, own])
+    whole, own, inner_gram = call(
+        deep_kernel,
+        [((ROWS, NODES), F32), ((HALF, 256), F32), ((2 * SNAPS, 2 * SNAPS), F32)],
+        [field, scales, low, const],
+    )
+    z_low, z_high = call(edge_kernel, [((Z_ROWS, 128), F32)] * 2, [left, right, low, own])
     before = pass_on(z_high, WIDE, 1)
     after = pass_on(z_low, WIDE, -1)
     gram = call(gram_kernel, [((near, 2, 128), F32)], [z_low, before, low, left, inner_gram])[0]
@@ -498,6 +566,13 @@
             ((SNAPS, SNAPS - 1), F32),
         ],
         [gram, whole, before, after, left, right, low],
+        scratch=[
+            pltpu.VMEM((SNAPS, 3, RADIAL, NODES), BF16),
+            pltpu.VMEM((SNAPS, SNAPS), F32),
+            pltpu.VMEM((SNAPS, SNAPS - 1), F32),
+            pltpu.SemaphoreType.DMA((2 + CHUNKS,)),
+        ],
+        hbm_out=True,
     )
     return (q_basis.reshape(velocity.shape), r_factor, dmd_operator)
 

time: 50.3 us -> 49.4 us (0.982)
  waiting for transfers between devices: 0.87 us -> 0.31 us
    ppermute x4, waiting for transfers between devices: 0.87 us -> 0.31 us  [pass_on(): lax.ppermute(x, axis, [(i, (i + step) % count) for i in range(count)])]
  transfers between devices with their start and end apart: 4 -> 4, of which waited for: 3 -> 2; matrix products, arithmetic and copies ran while one was open for 0% -> 0% of each run, Pallas kernels for 2% -> 2%
where the time goes in v3:
time: 49.4 us; the launch traced here: 49 us
  blocking collectives  22.7 us (46%)
  starting transfers between devices  20.6 us (42%)
  Pallas kernels  4.63 us (9%)
  between operations  0.69 us (1%)
    all_to_all x2, blocking collectives, from_everyone(): lax.all_to_all(copies, axis, split_axis=0, concat_axis=0, tiled=True, axi...  22.7 us
    ppermute x4, starting transfers between devices, pass_on(): lax.ppermute(x, axis, [(i, (i + step) % count) for i in range(count)])  20.6 us
    pallas_call x5, Pallas kernels, call(): pl.pallas_call(kernel, out_shape=[jax.ShapeDtypeStruct(shape, dtype) for...  4.63 us
  transfers between devices with their start and end apart: 4, of which 2 were waited for; matrix products, arithmetic and copies ran while one was open for 0% of the time, Pallas kernels for 2%

profile of v3, /device:TPU:1, one launch (start us, length us, event | category | flops | bytes accessed | tf_op | source)
XLA Modules:
  0.0 49.0 jit_solution(3041068829248955104)
XLA Ops:
  0.6 0.0 copy-start
  0.6 1.6 %shard_map.58 = (bf16[192,512]{1,0:T(8,128)(2,1)S(1)}, f32[16,128]{1,0:T(8,128)S(1)}, f32[104,128]{1,0:T(8,128)S(1)}, f32[104,128]{1,0:T(8,128)S(1)}) custom-call(bf16[16,3,4,512]{3,2,1,0:T(4,128)(2,1)} %bitcast.5, f32[3,1,4]{2,1,0:T(1,128)} %bitcast.6, f32[8,1152]{1,0:T(8,128)} %constant.4.clone.const_hbm.const_ref), custom_call_target="tpu_custom_call" | custom-call | tf_op jit(solution)/shard_map/pallas_call | solution.py:499
  2.3 2.7 %collective-permute-start = (f32[104,128]{1,0:T(8,128)S(1)}, f32[104,128]{1,0:T(8,128)S(1)}, u32[]{:S(2)}, u32[]{:S(2)}) collective-permute-start(f32[104,128]{1,0:T(8,128)S(1)} %get-tuple-element.17), channel_id=1, source_target_pairs={{0,1},{1,2},{2,3},{3,4},{4,5},{5,6},{6,7},{7,0},{8,9},{9,10},{10,1... | collective-permute-start | bytes 159752 | tf_op jit(solution)/shard_map/ppermute | solution.py:511
  4.9 4.2 %collective-permute-start.1 = (f32[104,128]{1,0:T(8,128)S(1)}, f32[104,128]{1,0:T(8,128)S(1)}, u32[]{:S(2)}, u32[]{:S(2)}) collective-permute-start(f32[104,128]{1,0:T(8,128)S(1)} %get-tuple-element.18.mine_ref.y_low_ref.refs_5_), channel_id=1, source_target_pairs={{0,7},{1,0},{2,1},{3,2},{4,3},{5,4},{6,5},{7,6},{8,15},{9,8},{10,9... | collective-permute-start | bytes 159752 | tf_op jit(solution)/shard_map/ppermute | solution.py:511
  9.1 0.0 copy-done
  9.1 0.8 %shard_map.59 = (f32[192,512]{1,0:T(8,128)S(1)}, f32[96,256]{1,0:T(8,128)S(1)}, f32[32,32]{1,0:T(8,128)S(1)}) custom-call(bf16[192,512]{1,0:T(8,128)(2,1)S(1)} %get-tuple-element.19.field_ref, f32[16,128]{1,0:T(8,128)S(1)} %get-tuple-element.20.scale_ref, f32[104,128]{1,0:T(8,128)S(1)} %get-tuple-element.18.mine_ref.y_low_ref.refs_5_, f32[8,1152]{1,0:T(8,128)S(1)} %copy-done), custom_call_target="tpu_custom_call" | custom-call | tf_op jit(solution)/shard_map/pallas_call | solution.py:499
  9.9 0.0 collective-permute-done.left_ref.refs_3_
  10.0 0.1 collective-permute-done.1.right_ref.refs_4_
  10.0 0.2 shard_map.60
  10.2 2.0 %collective-permute-start.2 = (f32[104,128]{1,0:T(8,128)S(1)}, f32[104,128]{1,0:T(8,128)S(1)}, u32[]{:S(2)}, u32[]{:S(2)}) collective-permute-start(f32[104,128]{1,0:T(8,128)S(1)} %get-tuple-element.23), channel_id=1, source_target_pairs={{0,8},{8,16},{16,24},{24,32},{32,40},{40,48},{48,56},{56,64},{64,7... | collective-permute-start | bytes 159752 | tf_op jit(solution)/shard_map/ppermute | solution.py:511
  12.3 11.7 %collective-permute-start.3 = (f32[104,128]{1,0:T(8,128)S(1)}, f32[104,128]{1,0:T(8,128)S(1)}, u32[]{:S(2)}, u32[]{:S(2)}) collective-permute-start(f32[104,128]{1,0:T(8,128)S(1)} %get-tuple-element.22.z_low_ref), channel_id=1, source_target_pairs={{0,504},{8,0},{16,8},{24,16},{32,24},{40,32},{48,40},{56,48},{64,5... | collective-permute-start | bytes 159752 | tf_op jit(solution)/shard_map/ppermute | solution.py:511
  24.0 0.2 collective-permute-done.2.before_ref.refs_1_
  24.2 0.4 shard_map.61
  24.6 9.5 %all_to_all.10 = f32[32,2,128]{2,1,0:T(2,128)S(1)} all-to-all(f32[32,2,128]{2,1,0:T(2,128)S(1)} %shard_map.61), channel_id=1, replica_groups={{261,262,263,384,385,386,387,388,389,390,391,0,1,2,3,4,5,6,7,128,129,13..., dimensions={0} | all-to-all | bytes 65536 | tf_op jit(solution)/shard_map/all_to_all | solution.py:517
  34.1 0.0 collective-permute-done.3.refs_2_
  34.1 13.2 %all_to_all.11.g_ref = f32[16,2,128]{2,1,0:T(2,128)S(1)} all-to-all(f32[16,2,128]{2,1,0:T(2,128)S(1)} %broadcast_in_dim.3), channel_id=1, replica_groups={{72,80,88,96,104,112,120,0,8,16,24,32,40,48,56,64},{73,81,89,97,105,113..., dimensions={0} | all-to-all | bytes 32768 | tf_op jit(solution)/shard_map/all_to_all | solution.py:517
  47.3 1.6 %shard_map.62 = (bf16[16,3,4,512]{3,2,1,0:T(4,128)(2,1)}, f32[16,16]{1,0:T(8,128)}, f32[16,15]{1,0:T(8,128)}) custom-call(f32[16,2,128]{2,1,0:T(2,128)S(1)} %all_to_all.11.g_ref, f32[192,512]{1,0:T(8,128)S(1)} %get-tuple-element.26.refs_0_, f32[104,128]{1,0:T(8,128)S(1)} %collective-permute-done.2.before_ref.refs_1_, ...), custom_call_target="tpu_custom_call" | custom-call | tf_op jit(solution)/shard_map/pallas_call | solution.py:499
  (2 shorter events, 0.0 us)
Async XLA Ops:
  0.6 8.5 %copy-start = (f32[8,1152]{1,0:T(8,128)S(1)}, f32[8,1152]{1,0:T(8,128)}, u32[]{:S(2)}) copy-start(f32[8,1152]{1,0:T(8,128)} %constant.4.clone.const_hbm.const_ref) | copy-start | bytes 110596
  2.3 7.7 %collective-permute-start = (f32[104,128]{1,0:T(8,128)S(1)}, f32[104,128]{1,0:T(8,128)S(1)}, u32[]{:S(2)}, u32[]{:S(2)}) collective-permute-start(f32[104,128]{1,0:T(8,128)S(1)} %get-tuple-element.17), channel_id=1, source_target_pairs={{0,1},{1,2},{2,3},{3,4},{4,5},{5,6},{6,7},{7,0},{8,9},{9,10},{10,1... | collective-permute-start | bytes 159752 | tf_op jit(solution)/shard_map/ppermute | solution.py:511
  4.9 5.1 %collective-permute-start.1 = (f32[104,128]{1,0:T(8,128)S(1)}, f32[104,128]{1,0:T(8,128)S(1)}, u32[]{:S(2)}, u32[]{:S(2)}) collective-permute-start(f32[104,128]{1,0:T(8,128)S(1)} %get-tuple-element.18.mine_ref.y_low_ref.refs_5_), channel_id=1, source_target_pairs={{0,7},{1,0},{2,1},{3,2},{4,3},{5,4},{6,5},{7,6},{8,15},{9,8},{10,9... | collective-permute-start | bytes 159752 | tf_op jit(solution)/shard_map/ppermute | solution.py:511
  10.2 14.0 %collective-permute-start.2 = (f32[104,128]{1,0:T(8,128)S(1)}, f32[104,128]{1,0:T(8,128)S(1)}, u32[]{:S(2)}, u32[]{:S(2)}) collective-permute-start(f32[104,128]{1,0:T(8,128)S(1)} %get-tuple-element.23), channel_id=1, source_target_pairs={{0,8},{8,16},{16,24},{24,32},{32,40},{40,48},{48,56},{56,64},{64,7... | collective-permute-start | bytes 159752 | tf_op jit(solution)/shard_map/ppermute | solution.py:511
  12.3 21.9 %collective-permute-start.3 = (f32[104,128]{1,0:T(8,128)S(1)}, f32[104,128]{1,0:T(8,128)S(1)}, u32[]{:S(2)}, u32[]{:S(2)}) collective-permute-start(f32[104,128]{1,0:T(8,128)S(1)} %get-tuple-element.22.z_low_ref), channel_id=1, source_target_pairs={{0,504},{8,0},{16,8},{24,16},{32,24},{40,32},{48,40},{56,48},{64,5... | collective-permute-start | bytes 159752 | tf_op jit(solution)/shard_map/ppermute | solution.py:511

commit v4 on v3

--- a/solution.py
+++ b/solution.py
@@ -184,10 +184,14 @@
     copies = [
         pltpu.make_async_copy(source, target, sems.at[i])
         for i, (source, target) in enumerate(
-            ((const_hbm, const_ref), (v_hbm, v_ref), (ext_hbm, ext_ref))
+            (
+                (const_hbm, const_ref),
+                (ext_hbm, ext_ref),
+                *((v_hbm.at[4 * k : 4 * k + 4], v_ref.at[4 * k : 4 * k + 4]) for k in range(4)),
+            )
         )
     ]
-    for copy in copies:
+    for copy in copies[2:] + copies[:2]:
         copy.start()
     permutation = to_slabs()
     lane = iota((1, 128), 1)
@@ -196,13 +200,14 @@
     copies[0].wait()
     base = [const_ref[:, NODES + 128 * k : NODES + 128 * k + 128] for k in range(2, 5)]
     d1, d2, d3 = face_derivatives(*base)
-    copies[1].wait()
+    for copy in copies[2:]:
+        copy.wait()
     flat = v_ref[...].reshape(ROWS, NODES)
     field = mm(permutation, flat).astype(BF16)
     field_ref[...] = field
     along1 = mm(field[64:], d1)
     others = mm(field, jnp.concatenate([d2, d3], axis=1))
-    copies[2].wait()
+    copies[1].wait()
     row8 = iota((8, 128), 0)
     volumes = jnp.zeros((8, 128), F32)
     faces = {}
@@ -541,7 +546,7 @@
             pltpu.VMEM((SNAPS, 3, RADIAL, NODES), BF16),
             pltpu.SMEM((3, 1, RADIAL), F32),
             pltpu.VMEM(const.shape, F32),
-            pltpu.SemaphoreType.DMA((3,)),
+            pltpu.SemaphoreType.DMA((6,)),
         ],
     )
     left = pass_on(high, NARROW, 1)

time: 49.4 us -> 49.4 us (level)
  no operation moved by 1% of the time
where the time goes in v4:
time: 49.4 us; the launch traced here: 48.9 us
  blocking collectives  22.7 us (46%)
  starting transfers between devices  20.6 us (42%)
  Pallas kernels  4.59 us (9%)
  between operations  0.69 us (1%)
    all_to_all x2, blocking collectives, from_everyone(): lax.all_to_all(copies, axis, split_axis=0, concat_axis=0, tiled=True, axi...  22.7 us
    ppermute x4, starting transfers between devices, pass_on(): lax.ppermute(x, axis, [(i, (i + step) % count) for i in range(count)])  20.6 us
    pallas_call x5, Pallas kernels, call(): pl.pallas_call(kernel, out_shape=[jax.ShapeDtypeStruct(shape, dtype) for...  4.59 us
  transfers between devices with their start and end apart: 4, of which 2 were waited for; matrix products, arithmetic and copies ran while one was open for 0% of the time, Pallas kernels for 2%

profile of v4, /device:TPU:1, one launch (start us, length us, event | category | flops | bytes accessed | tf_op | source)
XLA Modules:
  0.0 48.9 jit_solution(12776665527671100500)
XLA Ops:
  0.6 0.0 copy-start
  0.6 1.6 %shard_map.58 = (bf16[192,512]{1,0:T(8,128)(2,1)S(1)}, f32[16,128]{1,0:T(8,128)S(1)}, f32[104,128]{1,0:T(8,128)S(1)}, f32[104,128]{1,0:T(8,128)S(1)}) custom-call(bf16[16,3,4,512]{3,2,1,0:T(4,128)(2,1)} %bitcast.5, f32[3,1,4]{2,1,0:T(1,128)} %bitcast.6, f32[8,1152]{1,0:T(8,128)} %constant.4.clone.const_hbm.const_ref), custom_call_target="tpu_custom_call" | custom-call | tf_op jit(solution)/shard_map/pallas_call | solution.py:504
  2.2 2.7 %collective-permute-start = (f32[104,128]{1,0:T(8,128)S(1)}, f32[104,128]{1,0:T(8,128)S(1)}, u32[]{:S(2)}, u32[]{:S(2)}) collective-permute-start(f32[104,128]{1,0:T(8,128)S(1)} %get-tuple-element.17), channel_id=1, source_target_pairs={{0,1},{1,2},{2,3},{3,4},{4,5},{5,6},{6,7},{7,0},{8,9},{9,10},{10,1... | collective-permute-start | bytes 159752 | tf_op jit(solution)/shard_map/ppermute | solution.py:516
  4.9 4.2 %collective-permute-start.1 = (f32[104,128]{1,0:T(8,128)S(1)}, f32[104,128]{1,0:T(8,128)S(1)}, u32[]{:S(2)}, u32[]{:S(2)}) collective-permute-start(f32[104,128]{1,0:T(8,128)S(1)} %get-tuple-element.18.mine_ref.y_low_ref.refs_5_), channel_id=1, source_target_pairs={{0,7},{1,0},{2,1},{3,2},{4,3},{5,4},{6,5},{7,6},{8,15},{9,8},{10,9... | collective-permute-start | bytes 159752 | tf_op jit(solution)/shard_map/ppermute | solution.py:516
  9.1 0.0 copy-done
  9.1 0.8 %shard_map.59 = (f32[192,512]{1,0:T(8,128)S(1)}, f32[96,256]{1,0:T(8,128)S(1)}, f32[32,32]{1,0:T(8,128)S(1)}) custom-call(bf16[192,512]{1,0:T(8,128)(2,1)S(1)} %get-tuple-element.19.field_ref, f32[16,128]{1,0:T(8,128)S(1)} %get-tuple-element.20.scale_ref, f32[104,128]{1,0:T(8,128)S(1)} %get-tuple-element.18.mine_ref.y_low_ref.refs_5_, f32[8,1152]{1,0:T(8,128)S(1)} %copy-done), custom_call_target="tpu_custom_call" | custom-call | tf_op jit(solution)/shard_map/pallas_call | solution.py:504
  9.9 0.0 collective-permute-done.left_ref.refs_3_
  9.9 0.1 collective-permute-done.1.right_ref.refs_4_
  10.0 0.2 shard_map.60
  10.2 2.0 %collective-permute-start.2 = (f32[104,128]{1,0:T(8,128)S(1)}, f32[104,128]{1,0:T(8,128)S(1)}, u32[]{:S(2)}, u32[]{:S(2)}) collective-permute-start(f32[104,128]{1,0:T(8,128)S(1)} %get-tuple-element.23), channel_id=1, source_target_pairs={{0,8},{8,16},{16,24},{24,32},{32,40},{40,48},{48,56},{56,64},{64,7... | collective-permute-start | bytes 159752 | tf_op jit(solution)/shard_map/ppermute | solution.py:516
  12.2 11.7 %collective-permute-start.3 = (f32[104,128]{1,0:T(8,128)S(1)}, f32[104,128]{1,0:T(8,128)S(1)}, u32[]{:S(2)}, u32[]{:S(2)}) collective-permute-start(f32[104,128]{1,0:T(8,128)S(1)} %get-tuple-element.22.z_low_ref), channel_id=1, source_target_pairs={{0,504},{8,0},{16,8},{24,16},{32,24},{40,32},{48,40},{56,48},{64,5... | collective-permute-start | bytes 159752 | tf_op jit(solution)/shard_map/ppermute | solution.py:516
  23.9 0.2 collective-permute-done.2.before_ref.refs_1_
  24.1 0.4 shard_map.61
  24.5 9.5 %all_to_all.10 = f32[32,2,128]{2,1,0:T(2,128)S(1)} all-to-all(f32[32,2,128]{2,1,0:T(2,128)S(1)} %shard_map.61), channel_id=1, replica_groups={{261,262,263,384,385,386,387,388,389,390,391,0,1,2,3,4,5,6,7,128,129,13..., dimensions={0} | all-to-all | bytes 65536 | tf_op jit(solution)/shard_map/all_to_all | solution.py:522
  34.1 0.0 collective-permute-done.3.refs_2_
  34.1 13.2 %all_to_all.11.g_ref = f32[16,2,128]{2,1,0:T(2,128)S(1)} all-to-all(f32[16,2,128]{2,1,0:T(2,128)S(1)} %broadcast_in_dim.3), channel_id=1, replica_groups={{72,80,88,96,104,112,120,0,8,16,24,32,40,48,56,64},{73,81,89,97,105,113..., dimensions={0} | all-to-all | bytes 32768 | tf_op jit(solution)/shard_map/all_to_all | solution.py:522
  47.3 1.6 %shard_map.62 = (bf16[16,3,4,512]{3,2,1,0:T(4,128)(2,1)}, f32[16,16]{1,0:T(8,128)}, f32[16,15]{1,0:T(8,128)}) custom-call(f32[16,2,128]{2,1,0:T(2,128)S(1)} %all_to_all.11.g_ref, f32[192,512]{1,0:T(8,128)S(1)} %get-tuple-element.26.refs_0_, f32[104,128]{1,0:T(8,128)S(1)} %collective-permute-done.2.before_ref.refs_1_, ...), custom_call_target="tpu_custom_call" | custom-call | tf_op jit(solution)/shard_map/pallas_call | solution.py:504
  (2 shorter events, 0.0 us)
Async XLA Ops:
  0.6 8.5 %copy-start = (f32[8,1152]{1,0:T(8,128)S(1)}, f32[8,1152]{1,0:T(8,128)}, u32[]{:S(2)}) copy-start(f32[8,1152]{1,0:T(8,128)} %constant.4.clone.const_hbm.const_ref) | copy-start | bytes 110596
  2.2 7.7 %collective-permute-start = (f32[104,128]{1,0:T(8,128)S(1)}, f32[104,128]{1,0:T(8,128)S(1)}, u32[]{:S(2)}, u32[]{:S(2)}) collective-permute-start(f32[104,128]{1,0:T(8,128)S(1)} %get-tuple-element.17), channel_id=1, source_target_pairs={{0,1},{1,2},{2,3},{3,4},{4,5},{5,6},{6,7},{7,0},{8,9},{9,10},{10,1... | collective-permute-start | bytes 159752 | tf_op jit(solution)/shard_map/ppermute | solution.py:516
  4.9 5.1 %collective-permute-start.1 = (f32[104,128]{1,0:T(8,128)S(1)}, f32[104,128]{1,0:T(8,128)S(1)}, u32[]{:S(2)}, u32[]{:S(2)}) collective-permute-start(f32[104,128]{1,0:T(8,128)S(1)} %get-tuple-element.18.mine_ref.y_low_ref.refs_5_), channel_id=1, source_target_pairs={{0,7},{1,0},{2,1},{3,2},{4,3},{5,4},{6,5},{7,6},{8,15},{9,8},{10,9... | collective-permute-start | bytes 159752 | tf_op jit(solution)/shard_map/ppermute | solution.py:516
  10.2 14.0 %collective-permute-start.2 = (f32[104,128]{1,0:T(8,128)S(1)}, f32[104,128]{1,0:T(8,128)S(1)}, u32[]{:S(2)}, u32[]{:S(2)}) collective-permute-start(f32[104,128]{1,0:T(8,128)S(1)} %get-tuple-element.23), channel_id=1, source_target_pairs={{0,8},{8,16},{16,24},{24,32},{32,40},{40,48},{48,56},{56,64},{64,7... | collective-permute-start | bytes 159752 | tf_op jit(solution)/shard_map/ppermute | solution.py:516
  12.2 21.9 %collective-permute-start.3 = (f32[104,128]{1,0:T(8,128)S(1)}, f32[104,128]{1,0:T(8,128)S(1)}, u32[]{:S(2)}, u32[]{:S(2)}) collective-permute-start(f32[104,128]{1,0:T(8,128)S(1)} %get-tuple-element.22.z_low_ref), channel_id=1, source_target_pairs={{0,504},{8,0},{16,8},{24,16},{32,24},{40,32},{48,40},{56,48},{64,5... | collective-permute-start | bytes 159752 | tf_op jit(solution)/shard_map/ppermute | solution.py:516
